TPU v7x, 32 devices: a whole 2x2x4 slice. The times are simulated.
32 devices in a mesh: walk: 4 (over x, core), pb: 8 (over z, y).
Axes of the slice: x: 2, y: 2, z: 4, core: 2. Of those that a mesh axis runs over, the one named last changes fastest.
Arguments:
- greens: bfloat16 [64, 64, 3072], P('walk', 'pb'), may hold values from -6 to 6
- cholesky: bfloat16 [32, 300, 3072], P('pb'), may hold values from -0.011962891 to 0.011962891
- slot_source: int32 [32], replicated, may hold values from 0 to 63, as said below
- block_transfer_index: int32 [32], P('pb'), may hold values from 0 to 15
- slot_multiplicity: int32 [32], P('pb'), may hold values from 0 to 3, as said below
- fields: float32 [64, 16, 300], P('walk'), may hold values from -6 to 6
- weight: float32 [64], P('walk'), may hold values from 0.2 to 5
Outputs:
- force_bias: float32 [64, 2, 4800], P('walk', None, 'pb')
- local_energy: float32 [64], P('walk')
- new_weight: float32 [64], P('walk')
- mixed_energy: float32 [], replicated
Inputs may be any that keep to these rules, and one draw needn't show every extreme that they name: `slot_source`: the Green's block of k-point k lies on index k // 8 of pb; with P = 8, slot j of pb index d (slot d * 4 + j) reads a block that lies on index (d + o_j) mod P of pb, where o_0 = 0, o_1 = P - 1, o_2 = 1, o_3 = P // 2. `slot_multiplicity`: 0 marks an empty slot; on each index of pb the live slots come first, and on some index all 4 slots are live.
All inputs are finite; a program needn't handle non-finite values.
Results may differ from a plain program's by a relative error of at most 0.0003.
Values may be sent and summed in bfloat16 or wider, within the bound.
A program may use at most 320 MiB of HBM per device.

v0:
```python
import jax
import jax.numpy as jnp
from jax import lax
from jax.sharding import PartitionSpec as P

ORBITAL_COUNT = 96
OCCUPIED_COUNT = 16
TRANSFER_COUNT = 16


sqrt_step = 0.05


def from_behind(array, axis, by):
    devices = lax.axis_size(axis)
    return lax.ppermute(array, axis, [(i, (i + by) % devices) for i in range(devices)])


def slot_terms(chol_flat, green_flat):
    vectors = chol_flat.shape[0]
    walkers = green_flat.shape[0]
    doubled = 2 * ORBITAL_COUNT
    chol_block = chol_flat.reshape(vectors, OCCUPIED_COUNT, doubled)
    green_rows = green_flat.reshape(walkers, OCCUPIED_COUNT, doubled)
    real_part = green_rows[..., :ORBITAL_COUNT]
    imag_part = green_rows[..., ORBITAL_COUNT:]
    stacked = jnp.stack(
        [jnp.concatenate([real_part, -imag_part], -1), jnp.concatenate([imag_part, real_part], -1)],
        0,
    )
    left_matrix = chol_block.reshape(vectors * OCCUPIED_COUNT, doubled)
    right_matrix = stacked.reshape(2 * walkers * OCCUPIED_COUNT, doubled)
    product = lax.dot_general(
        left_matrix, right_matrix, (((1,), (1,)), ((), ())), preferred_element_type=jnp.float32
    )
    product = product.reshape(vectors, OCCUPIED_COUNT, 2, walkers, OCCUPIED_COUNT)
    identity = jnp.eye(OCCUPIED_COUNT, dtype=jnp.float32)
    diagonal = jnp.einsum("nicwj,ij->wcn", product, identity)
    crossed = jnp.einsum("nicwj,njcwi->cw", product, product)
    return (diagonal, crossed[0] - crossed[1])


def per_walker(bias_part, field_part):
    shift_real = sqrt_step * bias_part[:, 0]
    shift_imag = sqrt_step * bias_part[:, 1]
    coulomb = 0.5 * jnp.sum(
        bias_part[:, 0] * bias_part[:, 0] - bias_part[:, 1] * bias_part[:, 1], axis=1
    )
    real_arg = jnp.sum(
        field_part * shift_real - 0.5 * (shift_real * shift_real - shift_imag * shift_imag), axis=1
    )
    imag_arg = jnp.sum(field_part * shift_imag - shift_real * shift_imag, axis=1)
    return (coulomb, real_arg, imag_arg)


def local(greens, cholesky, slot_source, block_transfer_index, slot_multiplicity, fields, weight):
    group_list = lax.axis_size("pb")
    own_index = lax.axis_index("pb")
    slots_here = cholesky.shape[0]
    vectors = cholesky.shape[1]
    kpoints_here = greens.shape[1]
    walkers = greens.shape[0]
    source_table = slot_source.reshape(group_list, slots_here)
    own_sources = lax.dynamic_index_in_dim(source_table, own_index, 0, keepdims=False)
    offset_list = [0, group_list - 1, 1, group_list // 2]
    received = []
    for slot_index in range(slots_here):
        offset = offset_list[slot_index]
        if offset == 0:
            block = lax.dynamic_index_in_dim(
                greens, own_sources[slot_index] % kpoints_here, 1, keepdims=False
            )
        else:
            requester = (own_index + group_list - offset) % group_list
            wanted = (
                lax.dynamic_index_in_dim(source_table, requester, 0, keepdims=False)[slot_index]
                % kpoints_here
            )
            outgoing = lax.dynamic_index_in_dim(greens, wanted, 1, keepdims=False)
            block = from_behind(outgoing, "pb", group_list - offset)
        received.append(block)
    bias = jnp.zeros((walkers, 2, TRANSFER_COUNT, vectors), jnp.float32)
    exchange_sum = jnp.zeros((walkers,), jnp.float32)

    def live_terms(operands):
        return slot_terms(operands[0], operands[1])

    def empty_terms(operands):
        return (jnp.zeros((walkers, 2, vectors), jnp.float32), jnp.zeros((walkers,), jnp.float32))

    for slot_index in range(slots_here):
        multiple_count = slot_multiplicity[slot_index]
        diagonal, crossed = lax.cond(
            multiple_count > 0,
            live_terms,
            empty_terms,
            (cholesky[slot_index], received[slot_index]),
        )
        scaled = multiple_count.astype(jnp.float32)
        factor = scaled * (jnp.arange(TRANSFER_COUNT) == block_transfer_index[slot_index]).astype(
            jnp.float32
        )
        bias = bias + factor[None, None, :, None] * diagonal[:, :, None, :]
        exchange_sum = exchange_sum + scaled * crossed
    flat_bias = bias.reshape(walkers, 2, TRANSFER_COUNT * vectors)
    flat_fields = fields.reshape(walkers, TRANSFER_COUNT * vectors)
    share_width = TRANSFER_COUNT * vectors // group_list
    total_bias, exchange_total = lax.psum((flat_bias, exchange_sum), "pb")
    coulomb, real_arg, imag_arg = per_walker(total_bias, flat_fields)
    bias_share = lax.dynamic_slice_in_dim(total_bias, own_index * share_width, share_width, 2)
    energy = coulomb - 0.5 * exchange_total
    new_weight = weight * jnp.exp(real_arg) * jnp.maximum(jnp.cos(imag_arg), 0.0)
    weighted_energy, weight_total = lax.psum((jnp.sum(weight * energy), jnp.sum(weight)), "walk")
    return (bias_share, energy, new_weight, weighted_energy / weight_total)


def solution(mesh):
    placed = (
        P("walk", "pb", None),
        P("pb", None, None),
        P(),
        P("pb"),
        P("pb"),
        P("walk", None, None),
        P("walk"),
    )
    return jax.shard_map(
        local,
        mesh=mesh,
        in_specs=placed,
        out_specs=(P("walk", None, "pb"), P("walk"), P("walk"), P()),
        check_vma=False,
    )
```

profile of v0, /device:TPU:0, one launch (start us, length us, event | category | flops | bytes accessed | tf_op | source)
XLA Modules:
  0.0 1029.0 jit_solution(11361290466341111547)
XLA Ops:
  7.3 0.7 reshape.129
  8.0 0.6 slice.124
  10.5 0.6 slice.127
  13.1 0.6 slice.130
  15.6 2.5 constant_dynamic-slice_fusion.5
  18.2 0.7 copy.94
  18.8 4.1 collective-permute-start.2
  22.9 0.7 copy.95
  23.6 2.3 collective-permute-start.1
  26.0 1.4 fusion.6
  32.6 1.5 fusion.5
  34.1 0.7 compare_select_fusion.1
  34.9 0.7 mul.208
  35.6 0.6 compare_select_fusion
  36.2 0.7 mul.216
  37.0 0.6 compare_select_fusion.2
  37.7 0.7 mul.200
  38.4 0.6 compare_select_fusion.3
  39.1 0.7 mul.192
  39.8 221.6 %conditional.4 = (f32[16,2,300]{0,1,2:T(2,128)S(1)}, f32[16]{0:T(128)S(1)}) conditional(s32[]{:T(128)} %bitcast.32, () %tuple.42, (pred[]{:T(512)}, bf16[16,8,3072]{2,1,0:T(8,128)(2,1)}, bf16[4,300,3072]{2,0,1:T(4,128)(2,1)}, s32[]{:T(128)}, s32[]{:T(128)}, /*index=5*/s32[]{:T(128)}, s32[]{:T(128)}) %tuple.63), branch_computations={%region_0.1_spmd, %region_1.2_spmd.clone.clone} | conditional | flops 954055808 | bytes 105791416 | solution.py:93
  39.8 1.6 copy.79
  41.9 5.3 copy.80
  47.2 1.4 slice.154
  48.6 4.1 reshape_squeeze.14
  52.8 5.2 convolution_bitcast_fusion.3
  57.9 44.4 %reshape.154 = f32[300,16,2,16,16]{4,3,2,1,0:T(8,128)} reshape(f32[4800,512]{1,0:T(8,128)} %convolution_bitcast_fusion.3) | data formatting | bytes 19660800 | tf_op jit(solution)/shard_map/cond/branch_1_fun/reshape | solution.py:36
  102.3 24.6 %multiply_reduce_fusion.7 = f32[300,2,16]{2,1,0:T(2,128)S(1)} fusion(f32[300,16,2,16,16]{4,3,2,1,0:T(8,128)} %reshape.154, f32[16,16]{1,0:T(8,128)S(1)} %fusion.3), kind=kLoop, calls=%fused_computation.31 | loop fusion | flops 4905600 | bytes 9869824 | tf_op jit(solution)/shard_map/cond/branch_1_fun/nicwj,ij->wcn/dot_general | solution.py:38
  127.0 86.4 %copy.83 = f32[2,16,16,16,300]{2,1,0,3,4:T(8,128)} copy(f32[2,16,16,16,300]{3,1,0,2,4:T(8,128)} %bitcast.56) | data formatting | bytes 19660800 | tf_op jit(solution)/shard_map/cond
  213.4 47.7 %multiply_reduce_fusion.6 = f32[2,16]{1,0:T(2,128)S(1)} fusion(f32[2,16,16,16,300]{2,1,0,3,4:T(8,128)} %copy.83, f32[300,16,2,16,16]{4,3,2,1,0:T(8,128)} %reshape.154), kind=kLoop, calls=%fused_computation.30 | loop fusion | flops 4915168 | bytes 19660928 | tf_op jit(solution)/shard_map/cond/branch_1_fun/nicwj,njcwi->cw/dot_general | solution.py:39
  261.6 1.7 mul.195
  263.4 0.8 copy.24
  264.2 3.9 conditional.6
  268.3 0.3 copy-done.11
  268.6 11.5 %conditional.7 = (f32[16,2,300]{0,1,2:T(2,128)S(1)}, f32[16]{0:T(128)S(1)}) conditional(s32[]{:T(128)} %bitcast.46, () %tuple.48, (bf16[16,3072]{1,0:T(8,128)(2,1)}, bf16[4,300,3072]{2,0,1:T(4,128)(2,1)}) %tuple.49), branch_computations={%region_6.7_spmd, %region_7.8_spmd} | conditional | flops 954055808 | bytes 104021840 | solution.py:93
  280.1 0.5 copy-done.13
  280.9 0.9 mul.219
  281.8 0.9 mul.211
  282.8 1.7 mul.203
  284.5 2.5 multiply_add_fusion
  287.0 663.7 %psum.29 = f32[16]{0:T(128)S(1)} all-reduce(f32[16]{0:T(128)S(1)} %multiply_add_fusion.1), channel_id=1, replica_groups=mesh['walk'=4,'pb'=8] {'pb'}, use_global_device_ids=true, to_apply=%region_10.11 | all-reduce | flops 16 | bytes 128 | tf_op jit(solution)/shard_map/psum | solution.py:108
  950.7 55.1 %all-reduce.3.cloned.1.call-done = f32[16,2,4800]{2,1,0:T(2,128)} async-done(((f32[16,2,4800]{2,1,0:T(2,128)}), f32[16,2,4800]{2,1,0:T(2,128)}) %all-reduce.3.cloned.1.call-update) | async-done | bytes 614416 | tf_op jit(solution)/shard_map/psum | solution.py:108
  1005.8 3.6 multiply_reduce_fusion.8
  1009.5 0.3 mul.235
  1009.7 0.3 mul.231
  1010.0 0.3 subtract_reduce_fusion.1
  1010.3 1.2 fusion.4
  1011.5 6.3 all-reduce
  1019.1 1.7 constant_dynamic-slice_fusion.7
  (62 shorter events, 2.1 us)
Async XLA Ops:
  7.2 998.7 %all-reduce.3.cloned.1.call-start = ((), (), s32[]{:S(2)}) async-start(), calls=%async_computation | async-start | bytes 1245184 | tf_op jit(solution)/shard_map/psum | solution.py:108
  18.8 249.4 %collective-permute-start.2 = (bf16[16,3072]{1,0:T(8,128)(2,1)}, bf16[16,3072]{1,0:T(8,128)(2,1)}, u32[]{:S(2)}, u32[]{:S(2)}) collective-permute-start(bf16[16,3072]{1,0:T(8,128)(2,1)} %bitcast.109), channel_id=1, source_target_pairs={{0,4},{1,5},{2,6},{3,7},{4,0},{5,1},{6,2},{7,3},{8,12},{9,13},{10,... | collective-permute-start | bytes 294920 | tf_op jit(solution)/shard_map/ppermute | solution.py:16
  23.6 240.6 %collective-permute-start.1 = (bf16[16,3072]{1,0:T(8,128)(2,1)}, bf16[16,3072]{1,0:T(8,128)(2,1)}, u32[]{:S(2)}, u32[]{:S(2)}) collective-permute-start(bf16[16,3072]{1,0:T(8,128)(2,1)} %bitcast.110), channel_id=1, source_target_pairs={{0,7},{1,0},{2,1},{3,2},{4,3},{5,4},{6,5},{7,6},{8,15},{9,8},{10,9... | collective-permute-start | bytes 294920 | tf_op jit(solution)/shard_map/ppermute | solution.py:16
  25.9 237.4 %collective-permute-start = (bf16[16,3072]{1,0:T(8,128)(2,1)S(1)}, bf16[16,3072]{1,0:T(8,128)(2,1)S(1)}, u32[]{:S(2)}, u32[]{:S(2)}) collective-permute-start(bf16[16,3072]{1,0:T(8,128)(2,1)S(1)} %bitcast.121), channel_id=1, source_target_pairs={{0,1},{1,2},{2,3},{3,4},{4,5},{5,6},{6,7},{7,0},{8,9},{9,10},{10,1... | collective-permute-start | bytes 294920 | tf_op jit(solution)/shard_map/ppermute | solution.py:16
  261.3 2.0 copy-start.7
  263.4 0.8 copy-start.9
  268.1 0.5 copy-start.11
  268.6 14.1 %copy-start.2 = (f32[16,2,300]{2,1,0:T(2,128)S(1)}, f32[16,2,300]{2,1,0:T(2,128)}, u32[]{:S(2)}) copy-start(f32[16,2,300]{2,1,0:T(2,128)} %copy.24) | copy-start | bytes 115204
  268.6 15.8 %copy-start = (f32[16,2,4800]{2,1,0:T(2,128)S(1)}, f32[16,2,4800]{2,1,0:T(2,128)}, u32[]{:S(2)}) copy-start(f32[16,2,4800]{2,1,0:T(2,128)} %mul.195) | copy-start | bytes 1843204
  268.6 15.8 %copy-start.3 = (f32[4800]{0:T(1024)S(1)}, f32[4800]{0:T(1024)}, u32[]{:S(2)}) copy-start(f32[4800]{0:T(1024)} %mul.208) | copy-start | bytes 57604
  268.6 15.8 %copy-start.4 = (f32[4800]{0:T(1024)S(1)}, f32[4800]{0:T(1024)}, u32[]{:S(2)}) copy-start(f32[4800]{0:T(1024)} %mul.216) | copy-start | bytes 57604
  268.6 15.8 %copy-start.5 = (f32[4800]{0:T(1024)S(1)}, f32[4800]{0:T(1024)}, u32[]{:S(2)}) copy-start(f32[4800]{0:T(1024)} %mul.200) | copy-start | bytes 57604
  280.1 0.5 copy-start.13
  280.6 6.4 copy-start.8
  280.6 6.4 copy-start.10
  280.6 6.4 copy-start.12
  280.6 729.4 %copy-start.1 = (f32[16,16,300]{2,1,0:T(8,128)S(1)}, f32[16,16,300]{2,1,0:T(8,128)}, u32[]{:S(2)}) copy-start(f32[16,16,300]{2,1,0:T(8,128)} %param.20) | copy-start | bytes 921604
  280.6 729.7 %copy-start.6 = (f32[16]{0:T(128)S(1)}, f32[16]{0:T(128)}, u32[]{:S(2)}) copy-start(f32[16]{0:T(128)} %param.21) | copy-start | bytes 196
  280.6 6.4 copy-start.14
Sparse Core Ops, SparseCore 0:
  287.1 718.6 all-reduce.2
where the time goes:
time: 1050 us; the launch traced here: 1030 us
  blocking collectives  670 us (64%)
  local copies, waits for them, and re-layouts  166 us (16%)
  other arithmetic  82.7 us (8%)
  waiting for transfers between devices  55.1 us (5%)
  between operations  28.3 us (3%)
  loops' own time  15.5 us (1%)
    psum x1, blocking collectives, local(): total_bias, exchange_total = lax.psum((flat_bias, exchange_sum), 'pb')  664 us
    cond x1, local copies, waits for them, and re-layouts  86.4 us
    psum x1, waiting for transfers between devices, local(): total_bias, exchange_total = lax.psum((flat_bias, exchange_sum), 'pb')  55.1 us
    dot_general x1, other arithmetic, slot_terms(): crossed = jnp.einsum('nicwj,njcwi->cw', product, product)  47.7 us
    reshape x1, local copies, waits for them, and re-layouts, slot_terms(): product.reshape(vectors, OCCUPIED_COUNT, 2, walkers, OCCUPIED_COUNT)  44.4 us
    dot_general x1, other arithmetic, slot_terms(): diagonal = jnp.einsum('nicwj,ij->wcn', product, identity)  24.6 us
  transfers between devices with their start and end apart: 4, of which 1 were waited for; matrix products, arithmetic and copies ran while one was open for 23% of the time, Pallas kernels for 0%

commit v1 on v0

v1 whole, which is shorter than its diff:
```python
import functools

import jax
import jax.numpy as jnp
import numpy as np
from jax import lax
from jax.experimental import pallas as pl
from jax.experimental.pallas import tpu as pltpu
from jax.sharding import PartitionSpec as P

ORBITAL_COUNT = 96
OCCUPIED_COUNT = 16
TRANSFER_COUNT = 16
SQRT_STEP = 0.05

DOUBLED = 2 * ORBITAL_COUNT
PAIR = 2 * DOUBLED
WINDOW = 256
SHIFT = PAIR - WINDOW
VMEM_LIMIT = 60 * 1024 * 1024
F32 = jnp.float32


def offsets_of(devices):
    return [0, devices - 1, 1, devices // 2]


def arrangement():
    table = np.zeros((2, WINDOW, 2, 2, WINDOW), np.float32)
    for parity in range(2):
        start = parity * (DOUBLED - SHIFT)
        for window in range(2):
            out = window * (DOUBLED - SHIFT)
            for q in range(ORBITAL_COUNT):
                re, im = start + q, start + ORBITAL_COUNT + q
                first, second = out + q, out + ORBITAL_COUNT + q
                table[parity, re, window, 0, first] = 1.0
                table[parity, im, window, 0, second] = -1.0
                table[parity, im, window, 1, first] = 1.0
                table[parity, re, window, 1, second] = 1.0
    return table.reshape(2, WINDOW, 4 * WINDOW)


def select_kernel(devices, source_ref, greens_ref, out_ref, wide, picked):
    me = lax.axis_index("pb")
    walkers, kpoints, _ = greens_ref.shape
    slots = out_ref.shape[0]
    for w in range(walkers):
        wide[w] = greens_ref[w].astype(F32)
    for slot in range(slots):
        requester = lax.rem(me + devices - offsets_of(devices)[slot], devices)
        index = lax.rem(source_ref[requester * slots + slot], kpoints)
        for w in range(walkers):
            picked[slot, w : w + 1, :] = wide[w, pl.ds(index, 1), :]
        out_ref[slot] = picked[slot].astype(out_ref.dtype)


def exchange_kernel(devices, mine_ref, out_ref, landed, send_sems, recv_sems):
    me = lax.axis_index("pb")
    slots = mine_ref.shape[0]
    offsets = offsets_of(devices)
    barrier = pltpu.get_barrier_semaphore()
    for slot in range(1, slots):
        pl.semaphore_signal(
            barrier,
            inc=1,
            device_id={"pb": lax.rem(me + devices - offsets[slot], devices)},
            device_id_type=pl.DeviceIdType.MESH,
        )
    pl.semaphore_wait(barrier, slots - 1)
    copies = []
    for slot in range(slots - 1, 0, -1):
        copy = pltpu.make_async_remote_copy(
            src_ref=mine_ref.at[slot],
            dst_ref=landed.at[slot - 1],
            send_sem=send_sems.at[slot - 1],
            recv_sem=recv_sems.at[slot - 1],
            device_id={"pb": lax.rem(me + devices - offsets[slot], devices)},
            device_id_type=pl.DeviceIdType.MESH,
        )
        copy.start()
        copies.append((slot, copy))
    out_ref[0] = mine_ref[0]
    for slot, copy in reversed(copies):
        copy.wait_recv()
        out_ref[slot] = landed[slot - 1]
    for slot, copy in copies:
        copy.wait_send()


def row_of(part, occupied, walkers):
    half = (OCCUPIED_COUNT // 2) * walkers
    return part * 2 * half + (occupied % 2) * half + (occupied // 2) * walkers


def compute_kernel(
    transfer_ref, multiple_ref, green_ref, chol_ref, table_ref, dense_ref, cross_ref, operand, product, diagonal, crossed
):
    slot = pl.program_id(0)
    slots = pl.num_programs(0)
    walkers = green_ref.shape[1]
    vectors = chol_ref.shape[1]
    half = (OCCUPIED_COUNT // 2) * walkers
    pairs = OCCUPIED_COUNT // 2
    scaled = multiple_ref[slot].astype(F32)

    for parity in range(2):
        rows = jnp.concatenate(
            [green_ref[0, :, PAIR * p + SHIFT * parity : PAIR * p + SHIFT * parity + WINDOW] for p in range(pairs)], 0
        )
        spread = jnp.dot(rows, table_ref[parity], preferred_element_type=F32).astype(operand.dtype)
        for window in range(2):
            for part in range(2):
                at = (window * 2 + part) * WINDOW
                operand[window, pl.ds(part * 2 * half + parity * half, half), :] = spread[:, at : at + WINDOW]

    for i in range(OCCUPIED_COUNT):
        start = PAIR * (i // 2) + SHIFT * (i % 2)
        product[i] = lax.dot_general(
            operand[i % 2],
            chol_ref[0, :, start : start + WINDOW],
            (((1,), (1,)), ((), ())),
            preferred_element_type=F32,
        )

    def block(i, j, part):
        return product[i, pl.ds(row_of(part, j, walkers), walkers), :]

    zero = jnp.zeros((walkers, vectors), F32)
    off = [zero, zero]
    own = [zero, zero]
    trace = [zero, zero]
    for i in range(OCCUPIED_COUNT):
        for part in range(2):
            here = block(i, i, part)
            own[part] = own[part] + here * here
            trace[part] = trace[part] + here
            for j in range(i):
                off[part] = off[part] + block(i, j, part) * block(j, i, part)
    for part in range(2):
        diagonal[slot, part] = scaled * trace[part]
    total = scaled * ((own[0] - own[1]) + 2.0 * (off[0] - off[1]))

    @pl.when(slot == 0)
    def _():
        crossed[...] = total

    @pl.when(slot > 0)
    def _():
        crossed[...] += total

    @pl.when(slot == slots - 1)
    def _():
        held = diagonal.shape[0]
        cross_ref[...] = jnp.sum(crossed[...], axis=1, keepdims=True)
        shares, _, _, width = dense_ref.shape
        for t in range(TRANSFER_COUNT):
            keep = [(transfer_ref[s] == t).astype(jnp.int32).astype(F32) for s in range(held)]
            for part in range(2):
                value = keep[0] * diagonal[0, part]
                for s in range(1, held):
                    value = value + keep[s] * diagonal[s, part]
                low, high = t * vectors, (t + 1) * vectors
                for share in range(low // width, (high - 1) // width + 1):
                    first, last = max(low, share * width), min(high, (share + 1) * width)
                    dense_ref[share, part, :, first - share * width : last - share * width] = value[
                        :, first - low : last - low
                    ]


def reduce_kernel(
    devices,
    groups,
    dense_ref,
    cross_ref,
    field_ref,
    weight_ref,
    bias_ref,
    energy_ref,
    new_ref,
    mixed_ref,
    landed,
    own_sums,
    other_sums,
    own_mean,
    other_mean,
    share_send,
    share_recv,
    sum_send,
    sum_recv,
    mean_send,
    mean_recv,
):
    me = lax.axis_index("pb")
    group = lax.axis_index("walk")
    walkers = weight_ref.shape[1]

    def pb_peer(step):
        return {"pb": lax.rem(me + step, devices)}

    def walk_peer(step):
        return {"walk": lax.rem(group + step, groups)}

    barrier = pltpu.get_barrier_semaphore()
    for step in range(1, devices):
        pl.semaphore_signal(barrier, inc=1, device_id=pb_peer(step), device_id_type=pl.DeviceIdType.MESH)
    for step in range(1, groups):
        pl.semaphore_signal(barrier, inc=1, device_id=walk_peer(step), device_id_type=pl.DeviceIdType.MESH)
    pl.semaphore_wait(barrier, devices + groups - 2)

    def send_all(source_of, target, send_sems, recv_sems, peer, count):
        copies = []
        for step in range(1, count):
            copy = pltpu.make_async_remote_copy(
                src_ref=source_of(step),
                dst_ref=target.at[step - 1],
                send_sem=send_sems.at[step - 1],
                recv_sem=recv_sems.at[step - 1],
                device_id=peer(step),
                device_id_type=pl.DeviceIdType.MESH,
            )
            copy.start()
            copies.append(copy)
        return copies

    shares = send_all(
        lambda step: dense_ref.at[lax.rem(me + step, devices)], landed, share_send, share_recv, pb_peer, devices
    )
    row = lax.broadcasted_iota(jnp.int32, (walkers, walkers), 0)
    column = lax.broadcasted_iota(jnp.int32, (walkers, walkers), 1)
    same = row == column
    weight = jnp.sum(jnp.where(same, jnp.broadcast_to(weight_ref[...], (walkers, walkers)), 0.0), axis=1, keepdims=True)
    real, imag = dense_ref[me, 0], dense_ref[me, 1]
    for step in range(1, devices):
        shares[step - 1].wait_recv()
        real = real + landed[step - 1, 0]
        imag = imag + landed[step - 1, 1]
    bias_ref[:, 0, :] = real
    bias_ref[:, 1, :] = imag
    shift_real = SQRT_STEP * real
    shift_imag = SQRT_STEP * imag
    field = field_ref[...]
    coulomb = 0.5 * jnp.sum(real * real - imag * imag, axis=1, keepdims=True)
    real_arg = jnp.sum(
        field * shift_real - 0.5 * (shift_real * shift_real - shift_imag * shift_imag), axis=1, keepdims=True
    )
    imag_arg = jnp.sum(field * shift_imag - shift_real * shift_imag, axis=1, keepdims=True)
    lane = lax.broadcasted_iota(jnp.int32, own_sums.shape, 1)
    energy_part = coulomb - 0.5 * cross_ref[...]
    packed = jnp.where(lane == 0, energy_part, jnp.where(lane == 1, real_arg, jnp.where(lane == 2, imag_arg, 0.0)))
    own_sums[...] = packed
    sums = send_all(lambda step: own_sums, other_sums, sum_send, sum_recv, pb_peer, devices)
    for step in range(1, devices):
        sums[step - 1].wait_recv()
    total = jnp.zeros_like(packed)
    for index in range(devices):
        step = lax.rem(me + devices - index, devices)
        arrived = other_sums[jnp.maximum(step - 1, 0)]
        total = total + jnp.where(step == 0, packed, arrived)
    energy = jnp.sum(jnp.where(lane == 0, total, 0.0), axis=1, keepdims=True)
    full_real = jnp.sum(jnp.where(lane == 1, total, 0.0), axis=1, keepdims=True)
    full_imag = jnp.sum(jnp.where(lane == 2, total, 0.0), axis=1, keepdims=True)
    weighted = jnp.sum(weight * energy, axis=0, keepdims=True)
    weights = jnp.sum(weight, axis=0, keepdims=True)
    lane = lax.broadcasted_iota(jnp.int32, own_mean.shape, 1)
    mean = jnp.where(lane == 0, weighted, jnp.where(lane == 1, weights, 0.0))
    own_mean[...] = mean
    means = send_all(lambda step: own_mean, other_mean, mean_send, mean_recv, walk_peer, groups)
    new_weight = weight * jnp.exp(full_real) * jnp.maximum(jnp.cos(full_imag), 0.0)
    energy_ref[...] = jnp.sum(jnp.where(same, energy, 0.0), axis=0, keepdims=True)
    new_ref[...] = jnp.sum(jnp.where(same, new_weight, 0.0), axis=0, keepdims=True)
    for step in range(1, groups):
        means[step - 1].wait_recv()
    total = jnp.zeros_like(mean)
    for index in range(groups):
        step = lax.rem(group + groups - index, groups)
        arrived = other_mean[jnp.maximum(step - 1, 0)]
        total = total + jnp.where(step == 0, mean, arrived)
    upper = jnp.sum(jnp.where(lane == 0, total, 0.0)[:1], axis=1, keepdims=True)
    lower = jnp.sum(jnp.where(lane == 1, total, 0.0)[:1], axis=1, keepdims=True)
    mixed_ref[...] = upper / lower
    for copy in shares + sums + means:
        copy.wait_send()


def local(greens, cholesky, slot_source, block_transfer_index, slot_multiplicity, fields, weight):
    devices = lax.axis_size("pb")
    groups = lax.axis_size("walk")
    me = lax.axis_index("pb")
    walkers, kpoints, flat = greens.shape
    slots, vectors, _ = cholesky.shape
    width = TRANSFER_COUNT * vectors // devices
    vmem = pl.BlockSpec(memory_space=pltpu.VMEM)
    smem = pl.BlockSpec(memory_space=pltpu.SMEM)

    outgoing = pl.pallas_call(
        functools.partial(select_kernel, devices),
        out_shape=jax.ShapeDtypeStruct((slots, walkers, flat), greens.dtype),
        in_specs=[smem, vmem],
        out_specs=vmem,
        scratch_shapes=[pltpu.VMEM((walkers, kpoints, flat), F32), pltpu.VMEM((slots, walkers, flat), F32)],
        compiler_params=pltpu.CompilerParams(vmem_limit_bytes=VMEM_LIMIT),
        name="select",
    )(slot_source, greens)

    blocks = pl.pallas_call(
        functools.partial(exchange_kernel, devices),
        out_shape=jax.ShapeDtypeStruct((slots, walkers, flat), greens.dtype),
        in_specs=[vmem],
        out_specs=vmem,
        scratch_shapes=[
            pltpu.VMEM((slots - 1, walkers, flat), greens.dtype),
            pltpu.SemaphoreType.DMA((slots - 1,)),
            pltpu.SemaphoreType.DMA((slots - 1,)),
        ],
        compiler_params=pltpu.CompilerParams(collective_id=0, has_side_effects=True),
        name="exchange",
    )(outgoing)

    rows = 2 * OCCUPIED_COUNT * walkers
    dense, cross = pl.pallas_call(
        compute_kernel,
        grid=(slots,),
        out_shape=(
            jax.ShapeDtypeStruct((devices, 2, walkers, width), F32),
            jax.ShapeDtypeStruct((walkers, 1), F32),
        ),
        in_specs=[
            smem,
            smem,
            pl.BlockSpec((1, walkers, flat), lambda s: (s, 0, 0)),
            pl.BlockSpec((1, vectors, flat), lambda s: (s, 0, 0)),
            pl.BlockSpec((2, WINDOW, 4 * WINDOW), lambda s: (0, 0, 0)),
        ],
        out_specs=(
            pl.BlockSpec((devices, 2, walkers, width), lambda s: (0, 0, 0, 0)),
            pl.BlockSpec((walkers, 1), lambda s: (0, 0)),
        ),
        scratch_shapes=[
            pltpu.VMEM((2, rows, WINDOW), greens.dtype),
            pltpu.VMEM((OCCUPIED_COUNT, rows, vectors), F32),
            pltpu.VMEM((slots, 2, walkers, vectors), F32),
            pltpu.VMEM((walkers, vectors), F32),
        ],
        compiler_params=pltpu.CompilerParams(
            dimension_semantics=("arbitrary",), vmem_limit_bytes=VMEM_LIMIT
        ),
        name="terms",
    )(block_transfer_index, slot_multiplicity, blocks, cholesky, jnp.asarray(arrangement(), greens.dtype))

    if width % vectors == 0:
        each = width // vectors
        field_share = lax.dynamic_slice_in_dim(fields, me * each, each, 1).reshape(walkers, width)
    else:
        flat_fields = fields.reshape(walkers, TRANSFER_COUNT * vectors)
        field_share = lax.dynamic_slice_in_dim(flat_fields, me * width, width, 1)

    bias, energy, new_weight, mixed = pl.pallas_call(
        functools.partial(reduce_kernel, devices, groups),
        out_shape=(
            jax.ShapeDtypeStruct((walkers, 2, width), F32),
            jax.ShapeDtypeStruct((1, walkers), F32),
            jax.ShapeDtypeStruct((1, walkers), F32),
            jax.ShapeDtypeStruct((1, 1), F32),
        ),
        in_specs=[vmem] * 4,
        out_specs=(vmem,) * 4,
        scratch_shapes=[
            pltpu.VMEM((devices - 1, 2, walkers, width), F32),
            pltpu.VMEM((walkers, 128), F32),
            pltpu.VMEM((devices - 1, walkers, 128), F32),
            pltpu.VMEM((8, 128), F32),
            pltpu.VMEM((groups - 1, 8, 128), F32),
            pltpu.SemaphoreType.DMA((devices - 1,)),
            pltpu.SemaphoreType.DMA((devices - 1,)),
            pltpu.SemaphoreType.DMA((devices - 1,)),
            pltpu.SemaphoreType.DMA((devices - 1,)),
            pltpu.SemaphoreType.DMA((groups - 1,)),
            pltpu.SemaphoreType.DMA((groups - 1,)),
        ],
        compiler_params=pltpu.CompilerParams(collective_id=1, has_side_effects=True, vmem_limit_bytes=VMEM_LIMIT),
        name="reduce",
    )(dense, cross, field_share, weight.reshape(1, walkers))
    return (bias, energy.reshape(walkers), new_weight.reshape(walkers), mixed.reshape(()))


def solution(mesh):
    placed = (
        P("walk", "pb", None),
        P("pb", None, None),
        P(),
        P("pb"),
        P("pb"),
        P("walk", None, None),
        P("walk"),
    )
    return jax.shard_map(
        local,
        mesh=mesh,
        in_specs=placed,
        out_specs=(P("walk", None, "pb"), P("walk"), P("walk"), P()),
        check_vma=False,
    )
```

time: 1050 us -> 74.4 us (0.07); the launches traced: 1030 us -> 74.1 us
  blocking collectives: 670 us -> 0 us
  local copies, waits for them, and re-layouts: 166 us -> 12.8 us
  other arithmetic: 82.7 us -> 0 us
  Pallas kernels: 0 us -> 59 us
  waiting for transfers between devices: 55.1 us -> 0 us
  between operations: 28.3 us -> 2.34 us
  loops' own time: 15.5 us -> 0 us
    psum x2 -> x0, blocking collectives: 670 us -> none  [the longest x1 664 us: local(): total_bias, exchange_total = lax.psum((flat_bias, exchange_sum), 'pb')]
    cond x5 -> x0, local copies, waits for them, and re-layouts: 87.6 us -> none
    dot_general x2 -> x0, other arithmetic: 72.4 us -> none  [the longest x1 47.7 us: slot_terms(): crossed = jnp.einsum('nicwj,njcwi->cw', product, product)]
    pallas_call x0 -> x4, Pallas kernels: none -> 59 us  [the longest x1 30.2 us: local(): pl.pallas_call(functools.partial(reduce_kernel, devices, groups), out_sha...]
    psum x1 -> x0, waiting for transfers between devices: 55.1 us -> none  [local(): total_bias, exchange_total = lax.psum((flat_bias, exchange_sum), 'pb')]
    reshape x3 -> x1, local copies, waits for them, and re-layouts: 45.3 us -> 0.71 us  [local(): lax.dynamic_slice_in_dim(fields, me * each, each, 1).reshape(walkers, width)]
    another operation x4 -> x0, loops' own time: 15.5 us -> none  [local(): lax.cond(multiple_count > 0, live_terms, empty_terms, (cholesky[slot_inde...]
    another operation x9 -> x0, local copies, waits for them, and re-layouts: 11.3 us -> none
  transfers between devices with their start and end apart: 4 -> 0, of which waited for: 1 -> 0; matrix products, arithmetic and copies ran while one was open for 23% -> 0% of each run, Pallas kernels for 0% -> 0%
where the time goes in v1:
time: 74.4 us; the launch traced here: 74.1 us
  Pallas kernels  59 us (79%)
  local copies, waits for them, and re-layouts  12.8 us (17%)
  between operations  2.34 us (3%)
    pallas_call x1, Pallas kernels, local(): pl.pallas_call(functools.partial(reduce_kernel, devices, groups), out_sha...  30.2 us
    pallas_call x1, Pallas kernels, local(): pl.pallas_call(compute_kernel, grid=(slots,), out_shape=(jax.ShapeDtypeSt...  13.4 us
    pallas_call x1, Pallas kernels, local(): pl.pallas_call(functools.partial(exchange_kernel, devices), out_shape=jax...  13.1 us
    unnamed x6, local copies, waits for them, and re-layouts  12.1 us
    pallas_call x1, Pallas kernels, local(): pl.pallas_call(functools.partial(select_kernel, devices), out_shape=jax.S...  2.29 us

profile of v1, /device:TPU:0, one launch (start us, length us, event | category | flops | bytes accessed | tf_op | source)
XLA Modules:
  0.0 74.1 jit_solution(8378436641026692504)
XLA Ops:
  0.6 0.0 copy-start
  0.6 2.3 %select.1.mine_ref = bf16[4,16,3072]{2,1,0:T(8,128)(2,1)} custom-call(s32[32]{0:T(128)} %source_ref.1, bf16[16,8,3072]{2,1,0:T(8,128)(2,1)} %greens_ref.1), custom_call_target="tpu_custom_call" | custom-call | tf_op jit(solution)/shard_map/select/pallas_call | solution.py:296
  2.9 13.1 %exchange.1.green_ref = bf16[4,16,3072]{2,1,0:T(8,128)(2,1)} custom-call(bf16[4,16,3072]{2,1,0:T(8,128)(2,1)} %select.1.mine_ref), custom_call_target="tpu_custom_call" | custom-call | tf_op jit(solution)/shard_map/exchange/pallas_call | solution.py:306
  16.1 8.3 %copy.13.chol_ref = bf16[4,300,3072]{2,1,0:T(8,128)(2,1)} copy(bf16[4,300,3072]{2,0,1:T(4,128)(2,1)} %param.9) | data formatting | bytes 14745600 | tf_op args[1]
  24.4 13.4 %terms.1 = (f32[8,2,16,600]{3,2,1,0:T(8,128)}, f32[16,1]{1,0:T(8,128)}) custom-call(s32[4]{0:T(128)} %transfer_ref.1, s32[4]{0:T(128)} %multiple_ref.1, bf16[4,16,3072]{2,1,0:T(8,128)(2,1)} %exchange.1.green_ref, bf16[4,300,3072]{2,1,0:T(8,128)(2,1)} %copy.13.chol_ref, bf16[2,256,1024]{2,1,0:T(8,128)(2,1)} %constant.12.clone.table_ref), custom_call_target="tpu_custom_call" | custom-call | tf_op jit(solution)/shard_map/terms/pallas_call | solution.py:321
  37.8 0.0 copy-done
  37.8 0.7 reshape.23.field_ref
  38.5 30.2 %reduce.1 = (f32[16,2,600]{2,1,0:T(2,128)}, f32[1,16]{1,0:T(1,128)}, f32[1,16]{1,0:T(1,128)}, f32[1,1]{1,0:T(1,128)}) custom-call(f32[8,2,16,600]{3,2,1,0:T(8,128)} %get-tuple-element.10.dense_ref, f32[16,1]{1,0:T(8,128)} %get-tuple-element.11.cross_ref, f32[16,600]{1,0:T(8,128)} %reshape.23.field_ref, f32[1,16]{1,0:T(1,128)} %bitcast.4), custom_call_target="tpu_custom_call" | custom-call | tf_op jit(solution)/shard_map/reduce/pallas_call | solution.py:358
  68.7 1.5 %copy.18 = f32[16,2,600]{2,1,0:T(2,128)} copy(f32[16,2,600]{2,1,0:T(2,128)} %get-tuple-element.20) | data formatting | bytes 153600
  70.2 1.1 %copy.19 = f32[16]{0:T(128)} copy(f32[16]{0:T(128)} %bitcast.6) | data formatting | bytes 128
  71.3 1.1 %copy.20 = f32[16]{0:T(128)} copy(f32[16]{0:T(128)} %bitcast.5) | data formatting | bytes 128
  (1 shorter events, 0.0 us)
Async XLA Ops:
  0.6 37.1 %copy-start = (f32[16,16,300]{2,1,0:T(8,128)S(1)}, f32[16,16,300]{2,1,0:T(8,128)}, u32[]{:S(2)}) copy-start(f32[16,16,300]{2,1,0:T(8,128)} %param.13) | copy-start | bytes 921604

commit v2 on v1

--- a/solution.py
+++ b/solution.py
@@ -41,10 +41,11 @@
     return table.reshape(2, WINDOW, 4 * WINDOW)
 
 
-def select_kernel(devices, source_ref, greens_ref, out_ref, wide, picked):
+def select_kernel(devices, source_ref, greens_ref, *rest):
     me = lax.axis_index("pb")
     walkers, kpoints, _ = greens_ref.shape
-    slots = out_ref.shape[0]
+    outs, (wide, picked) = rest[:-2], rest[-2:]
+    slots = len(outs)
     for w in range(walkers):
         wide[w] = greens_ref[w].astype(F32)
     for slot in range(slots):
@@ -52,40 +53,7 @@
         index = lax.rem(source_ref[requester * slots + slot], kpoints)
         for w in range(walkers):
             picked[slot, w : w + 1, :] = wide[w, pl.ds(index, 1), :]
-        out_ref[slot] = picked[slot].astype(out_ref.dtype)
-
-
-def exchange_kernel(devices, mine_ref, out_ref, landed, send_sems, recv_sems):
-    me = lax.axis_index("pb")
-    slots = mine_ref.shape[0]
-    offsets = offsets_of(devices)
-    barrier = pltpu.get_barrier_semaphore()
-    for slot in range(1, slots):
-        pl.semaphore_signal(
-            barrier,
-            inc=1,
-            device_id={"pb": lax.rem(me + devices - offsets[slot], devices)},
-            device_id_type=pl.DeviceIdType.MESH,
-        )
-    pl.semaphore_wait(barrier, slots - 1)
-    copies = []
-    for slot in range(slots - 1, 0, -1):
-        copy = pltpu.make_async_remote_copy(
-            src_ref=mine_ref.at[slot],
-            dst_ref=landed.at[slot - 1],
-            send_sem=send_sems.at[slot - 1],
-            recv_sem=recv_sems.at[slot - 1],
-            device_id={"pb": lax.rem(me + devices - offsets[slot], devices)},
-            device_id_type=pl.DeviceIdType.MESH,
-        )
-        copy.start()
-        copies.append((slot, copy))
-    out_ref[0] = mine_ref[0]
-    for slot, copy in reversed(copies):
-        copy.wait_recv()
-        out_ref[slot] = landed[slot - 1]
-    for slot, copy in copies:
-        copy.wait_send()
+        outs[slot][...] = picked[slot].astype(greens_ref.dtype)
 
 
 def row_of(part, occupied, walkers):
@@ -94,19 +62,27 @@
 
 
 def compute_kernel(
-    transfer_ref, multiple_ref, green_ref, chol_ref, table_ref, dense_ref, cross_ref, operand, product, diagonal, crossed
+    transfer_ref, multiple_ref, chol_ref, table_ref, *rest
 ):
+    greens, (dense_ref, cross_ref, operand, product, diagonal, crossed, green) = rest[:-7], rest[-7:]
     slot = pl.program_id(0)
     slots = pl.num_programs(0)
-    walkers = green_ref.shape[1]
+    walkers = green.shape[0]
     vectors = chol_ref.shape[1]
     half = (OCCUPIED_COUNT // 2) * walkers
     pairs = OCCUPIED_COUNT // 2
     scaled = multiple_ref[slot].astype(F32)
 
+    for index, green_ref in enumerate(greens):
+
+        @pl.when(slot == index)
+        def _():
+            green[...] = green_ref[...]
+
+
     for parity in range(2):
         rows = jnp.concatenate(
-            [green_ref[0, :, PAIR * p + SHIFT * parity : PAIR * p + SHIFT * parity + WINDOW] for p in range(pairs)], 0
+            [green[:, PAIR * p + SHIFT * parity : PAIR * p + SHIFT * parity + WINDOW] for p in range(pairs)], 0
         )
         spread = jnp.dot(rows, table_ref[parity], preferred_element_type=F32).astype(operand.dtype)
         for window in range(2):
@@ -168,6 +144,20 @@
                     ]
 
 
+def on_diagonal(count):
+    return lax.broadcasted_iota(jnp.int32, (count, count), 0) == lax.broadcasted_iota(jnp.int32, (count, count), 1)
+
+
+def column_of(row):
+    count = row.shape[1]
+    return jnp.sum(jnp.where(on_diagonal(count), jnp.broadcast_to(row, (count, count)), 0.0), axis=1, keepdims=True)
+
+
+def row_from(column):
+    count = column.shape[0]
+    return jnp.sum(jnp.where(on_diagonal(count), jnp.broadcast_to(column, (count, count)), 0.0), axis=0, keepdims=True)
+
+
 def reduce_kernel(
     devices,
     groups,
@@ -176,9 +166,8 @@
     field_ref,
     weight_ref,
     bias_ref,
-    energy_ref,
-    new_ref,
-    mixed_ref,
+    total_ref,
+    mean_ref,
     landed,
     own_sums,
     other_sums,
@@ -226,17 +215,14 @@
     shares = send_all(
         lambda step: dense_ref.at[lax.rem(me + step, devices)], landed, share_send, share_recv, pb_peer, devices
     )
-    row = lax.broadcasted_iota(jnp.int32, (walkers, walkers), 0)
-    column = lax.broadcasted_iota(jnp.int32, (walkers, walkers), 1)
-    same = row == column
-    weight = jnp.sum(jnp.where(same, jnp.broadcast_to(weight_ref[...], (walkers, walkers)), 0.0), axis=1, keepdims=True)
+    weight = column_of(weight_ref[...])
     real, imag = dense_ref[me, 0], dense_ref[me, 1]
     for step in range(1, devices):
         shares[step - 1].wait_recv()
         real = real + landed[step - 1, 0]
         imag = imag + landed[step - 1, 1]
-    bias_ref[:, 0, :] = real
-    bias_ref[:, 1, :] = imag
+    bias_ref[0] = real
+    bias_ref[1] = imag
     shift_real = SQRT_STEP * real
     shift_imag = SQRT_STEP * imag
     field = field_ref[...]
@@ -257,18 +243,14 @@
         step = lax.rem(me + devices - index, devices)
         arrived = other_sums[jnp.maximum(step - 1, 0)]
         total = total + jnp.where(step == 0, packed, arrived)
+    total_ref[...] = total
     energy = jnp.sum(jnp.where(lane == 0, total, 0.0), axis=1, keepdims=True)
-    full_real = jnp.sum(jnp.where(lane == 1, total, 0.0), axis=1, keepdims=True)
-    full_imag = jnp.sum(jnp.where(lane == 2, total, 0.0), axis=1, keepdims=True)
     weighted = jnp.sum(weight * energy, axis=0, keepdims=True)
     weights = jnp.sum(weight, axis=0, keepdims=True)
     lane = lax.broadcasted_iota(jnp.int32, own_mean.shape, 1)
     mean = jnp.where(lane == 0, weighted, jnp.where(lane == 1, weights, 0.0))
     own_mean[...] = mean
     means = send_all(lambda step: own_mean, other_mean, mean_send, mean_recv, walk_peer, groups)
-    new_weight = weight * jnp.exp(full_real) * jnp.maximum(jnp.cos(full_imag), 0.0)
-    energy_ref[...] = jnp.sum(jnp.where(same, energy, 0.0), axis=0, keepdims=True)
-    new_ref[...] = jnp.sum(jnp.where(same, new_weight, 0.0), axis=0, keepdims=True)
     for step in range(1, groups):
         means[step - 1].wait_recv()
     total = jnp.zeros_like(mean)
@@ -276,11 +258,24 @@
         step = lax.rem(group + groups - index, groups)
         arrived = other_mean[jnp.maximum(step - 1, 0)]
         total = total + jnp.where(step == 0, mean, arrived)
-    upper = jnp.sum(jnp.where(lane == 0, total, 0.0)[:1], axis=1, keepdims=True)
-    lower = jnp.sum(jnp.where(lane == 1, total, 0.0)[:1], axis=1, keepdims=True)
-    mixed_ref[...] = upper / lower
+    mean_ref[...] = total
     for copy in shares + sums + means:
         copy.wait_send()
+
+
+def finish_kernel(sums_ref, total_ref, mean_ref, weight_ref, bias_ref, energy_ref, new_ref, mixed_ref):
+    bias_ref[:, 0, :] = sums_ref[0]
+    bias_ref[:, 1, :] = sums_ref[1]
+    total = total_ref[...]
+    weight = column_of(weight_ref[...])
+    lane = lax.broadcasted_iota(jnp.int32, total.shape, 1)
+    energy = jnp.sum(jnp.where(lane == 0, total, 0.0), axis=1, keepdims=True)
+    real = jnp.sum(jnp.where(lane == 1, total, 0.0), axis=1, keepdims=True)
+    imag = jnp.sum(jnp.where(lane == 2, total, 0.0), axis=1, keepdims=True)
+    energy_ref[...] = row_from(energy)
+    new_ref[...] = row_from(weight * jnp.exp(real) * jnp.maximum(jnp.cos(imag), 0.0))
+    mean = mean_ref[:1, :]
+    mixed_ref[...] = mean[:, 0:1] / mean[:, 1:2]
 
 
 def local(greens, cholesky, slot_source, block_transfer_index, slot_multiplicity, fields, weight):
@@ -295,27 +290,18 @@
 
     outgoing = pl.pallas_call(
         functools.partial(select_kernel, devices),
-        out_shape=jax.ShapeDtypeStruct((slots, walkers, flat), greens.dtype),
+        out_shape=(jax.ShapeDtypeStruct((walkers, flat), greens.dtype),) * slots,
         in_specs=[smem, vmem],
-        out_specs=vmem,
+        out_specs=(vmem,) * slots,
         scratch_shapes=[pltpu.VMEM((walkers, kpoints, flat), F32), pltpu.VMEM((slots, walkers, flat), F32)],
         compiler_params=pltpu.CompilerParams(vmem_limit_bytes=VMEM_LIMIT),
         name="select",
     )(slot_source, greens)
 
-    blocks = pl.pallas_call(
-        functools.partial(exchange_kernel, devices),
-        out_shape=jax.ShapeDtypeStruct((slots, walkers, flat), greens.dtype),
-        in_specs=[vmem],
-        out_specs=vmem,
-        scratch_shapes=[
-            pltpu.VMEM((slots - 1, walkers, flat), greens.dtype),
-            pltpu.SemaphoreType.DMA((slots - 1,)),
-            pltpu.SemaphoreType.DMA((slots - 1,)),
-        ],
-        compiler_params=pltpu.CompilerParams(collective_id=0, has_side_effects=True),
-        name="exchange",
-    )(outgoing)
+    arrived = [outgoing[0]]
+    for slot in range(1, slots):
+        by = devices - offsets_of(devices)[slot]
+        arrived.append(lax.ppermute(outgoing[slot], "pb", [(i, (i + by) % devices) for i in range(devices)]))
 
     rows = 2 * OCCUPIED_COUNT * walkers
     dense, cross = pl.pallas_call(
@@ -328,10 +314,10 @@
         in_specs=[
             smem,
             smem,
-            pl.BlockSpec((1, walkers, flat), lambda s: (s, 0, 0)),
             pl.BlockSpec((1, vectors, flat), lambda s: (s, 0, 0)),
             pl.BlockSpec((2, WINDOW, 4 * WINDOW), lambda s: (0, 0, 0)),
-        ],
+        ]
+        + [pl.BlockSpec((walkers, flat), lambda s: (0, 0))] * slots,
         out_specs=(
             pl.BlockSpec((devices, 2, walkers, width), lambda s: (0, 0, 0, 0)),
             pl.BlockSpec((walkers, 1), lambda s: (0, 0)),
@@ -341,12 +327,13 @@
             pltpu.VMEM((OCCUPIED_COUNT, rows, vectors), F32),
             pltpu.VMEM((slots, 2, walkers, vectors), F32),
             pltpu.VMEM((walkers, vectors), F32),
+            pltpu.VMEM((walkers, flat), greens.dtype),
         ],
         compiler_params=pltpu.CompilerParams(
             dimension_semantics=("arbitrary",), vmem_limit_bytes=VMEM_LIMIT
         ),
         name="terms",
-    )(block_transfer_index, slot_multiplicity, blocks, cholesky, jnp.asarray(arrangement(), greens.dtype))
+    )(block_transfer_index, slot_multiplicity, cholesky, jnp.asarray(arrangement(), greens.dtype), *arrived)
 
     if width % vectors == 0:
         each = width // vectors
@@ -355,16 +342,15 @@
         flat_fields = fields.reshape(walkers, TRANSFER_COUNT * vectors)
         field_share = lax.dynamic_slice_in_dim(flat_fields, me * width, width, 1)
 
-    bias, energy, new_weight, mixed = pl.pallas_call(
+    sums, total, mean = pl.pallas_call(
         functools.partial(reduce_kernel, devices, groups),
         out_shape=(
-            jax.ShapeDtypeStruct((walkers, 2, width), F32),
-            jax.ShapeDtypeStruct((1, walkers), F32),
-            jax.ShapeDtypeStruct((1, walkers), F32),
-            jax.ShapeDtypeStruct((1, 1), F32),
+            jax.ShapeDtypeStruct((2, walkers, width), F32),
+            jax.ShapeDtypeStruct((walkers, 128), F32),
+            jax.ShapeDtypeStruct((8, 128), F32),
         ),
         in_specs=[vmem] * 4,
-        out_specs=(vmem,) * 4,
+        out_specs=(vmem,) * 3,
         scratch_shapes=[
             pltpu.VMEM((devices - 1, 2, walkers, width), F32),
             pltpu.VMEM((walkers, 128), F32),
@@ -381,6 +367,19 @@
         compiler_params=pltpu.CompilerParams(collective_id=1, has_side_effects=True, vmem_limit_bytes=VMEM_LIMIT),
         name="reduce",
     )(dense, cross, field_share, weight.reshape(1, walkers))
+
+    bias, energy, new_weight, mixed = pl.pallas_call(
+        finish_kernel,
+        out_shape=(
+            jax.ShapeDtypeStruct((walkers, 2, width), F32),
+            jax.ShapeDtypeStruct((1, walkers), F32),
+            jax.ShapeDtypeStruct((1, walkers), F32),
+            jax.ShapeDtypeStruct((1, 1), F32),
+        ),
+        in_specs=[vmem] * 4,
+        out_specs=(vmem,) * 4,
+        name="finish",
+    )(sums, total, mean, weight.reshape(1, walkers))
     return (bias, energy.reshape(walkers), new_weight.reshape(walkers), mixed.reshape(()))
 
 

time: 74.4 us -> 63.6 us (0.85)
  Pallas kernels: 59 us -> 45.9 us
  starting transfers between devices: 0 us -> 6.99 us
  local copies, waits for them, and re-layouts: 12.8 us -> 9.78 us
  between operations: 2.34 us -> 0.68 us
    pallas_call x2, Pallas kernels: 15.4 us -> 3.86 us  [the longest x1 2.21 us: local(): pl.pallas_call(functools.partial(select_kernel, devices), out_shape=(jax....]
    ppermute x0 -> x3, starting transfers between devices: none -> 6.99 us  [local(): lax.ppermute(outgoing[slot], 'pb', [(i, (i + by) % devices) for i in rang...]
    unnamed x6 -> x9, local copies, waits for them, and re-layouts: 12.1 us -> 9.05 us
    pallas_call x1, Pallas kernels: 30.2 us -> 28.5 us  [local(): pl.pallas_call(functools.partial(reduce_kernel, devices, groups), out_sha...]
  transfers between devices with their start and end apart: 0 -> 3, of which waited for: 0 -> 0; matrix products, arithmetic and copies ran while one was open for 0% -> 14% of each run, Pallas kernels for 0% -> 0%
where the time goes in v2:
time: 63.6 us; the launch traced here: 63.3 us
  Pallas kernels  45.9 us (72%)
  local copies, waits for them, and re-layouts  9.78 us (15%)
  starting transfers between devices  6.99 us (11%)
  between operations  0.68 us (1%)
    pallas_call x1, Pallas kernels, local(): pl.pallas_call(functools.partial(reduce_kernel, devices, groups), out_sha...  28.5 us
    pallas_call x1, Pallas kernels, local(): pl.pallas_call(compute_kernel, grid=(slots,), out_shape=(jax.ShapeDtypeSt...  13.5 us
    unnamed x9, local copies, waits for them, and re-layouts  9.05 us
    ppermute x3, starting transfers between devices, local(): lax.ppermute(outgoing[slot], 'pb', [(i, (i + by) % devices) for i in rang...  6.99 us
    pallas_call x1, Pallas kernels, local(): pl.pallas_call(functools.partial(select_kernel, devices), out_shape=(jax....  2.21 us
    pallas_call x1, Pallas kernels, local(): pl.pallas_call(finish_kernel, out_shape=(jax.ShapeDtypeStruct((walkers, 2...  1.65 us
  transfers between devices with their start and end apart: 3, of which 0 were waited for; matrix products, arithmetic and copies ran while one was open for 14% of the time, Pallas kernels for 0%

profile of v2, /device:TPU:0, one launch (start us, length us, event | category | flops | bytes accessed | tf_op | source)
XLA Modules:
  0.0 63.3 jit_solution(17470897381046196267)
XLA Ops:
  0.6 0.0 copy-start
  0.6 2.2 %select.1 = (bf16[16,3072]{1,0:T(8,128)(2,1)}, bf16[16,3072]{1,0:T(8,128)(2,1)}, bf16[16,3072]{1,0:T(8,128)(2,1)}, bf16[16,3072]{1,0:T(8,128)(2,1)}) custom-call(s32[32]{0:T(128)} %source_ref.1, bf16[16,8,3072]{2,1,0:T(8,128)(2,1)} %greens_ref.1), custom_call_target="tpu_custom_call" | custom-call | tf_op jit(solution)/shard_map/select/pallas_call | solution.py:291
  2.9 3.0 %collective-permute-start = (bf16[16,3072]{1,0:T(8,128)(2,1)}, bf16[16,3072]{1,0:T(8,128)(2,1)S(1)}, u32[]{:S(2)}, u32[]{:S(2)}) collective-permute-start(bf16[16,3072]{1,0:T(8,128)(2,1)} %get-tuple-element.18), channel_id=1, source_target_pairs={{0,1},{1,2},{2,3},{3,4},{4,5},{5,6},{6,7},{7,0},{8,9},{9,10},{10,1... | collective-permute-start | bytes 294920 | tf_op jit(solution)/shard_map/ppermute | solution.py:304
  5.9 3.0 %collective-permute-start.1 = (bf16[16,3072]{1,0:T(8,128)(2,1)}, bf16[16,3072]{1,0:T(8,128)(2,1)S(1)}, u32[]{:S(2)}, u32[]{:S(2)}) collective-permute-start(bf16[16,3072]{1,0:T(8,128)(2,1)} %get-tuple-element.19), channel_id=1, source_target_pairs={{0,7},{1,0},{2,1},{3,2},{4,3},{5,4},{6,5},{7,6},{8,15},{9,8},{10,9... | collective-permute-start | bytes 294920 | tf_op jit(solution)/shard_map/ppermute | solution.py:304
  8.9 1.0 %collective-permute-start.2 = (bf16[16,3072]{1,0:T(8,128)(2,1)}, bf16[16,3072]{1,0:T(8,128)(2,1)S(1)}, u32[]{:S(2)}, u32[]{:S(2)}) collective-permute-start(bf16[16,3072]{1,0:T(8,128)(2,1)} %get-tuple-element.20), channel_id=1, source_target_pairs={{0,4},{1,5},{2,6},{3,7},{4,0},{5,1},{6,2},{7,3},{8,12},{9,13},{10,... | collective-permute-start | bytes 294920 | tf_op jit(solution)/shard_map/ppermute | solution.py:304
  9.8 8.3 %copy.13.chol_ref = bf16[4,300,3072]{2,1,0:T(8,128)(2,1)} copy(bf16[4,300,3072]{2,0,1:T(4,128)(2,1)} %param.9) | data formatting | bytes 14745600 | tf_op args[1]
  18.2 0.0 copy-done
  18.2 0.7 %reshape.24.field_ref = f32[16,600]{1,0:T(8,128)} reshape(f32[16,2,300]{2,1,0:T(2,128)S(1)} %constant_dynamic-slice_fusion) | data formatting | bytes 76800 | tf_op jit(solution)/shard_map/reshape | solution.py:340
  18.9 0.0 collective-permute-done.rest_1_
  18.9 0.0 copy-start.1
  18.9 0.0 collective-permute-done.1.rest_2_
  18.9 0.0 copy-start.2
  18.9 0.0 collective-permute-done.2.rest_3_
  19.0 0.0 copy-start.3
  19.0 0.6 copy-done.1
  19.6 0.0 copy-done.2
  19.6 0.1 copy-done.3
  19.7 13.5 %terms.1 = (f32[8,2,16,600]{3,2,1,0:T(8,128)}, f32[16,1]{1,0:T(8,128)}) custom-call(s32[4]{0:T(128)} %transfer_ref.1, s32[4]{0:T(128)} %multiple_ref.1, bf16[4,300,3072]{2,1,0:T(8,128)(2,1)} %copy.13.chol_ref, bf16[2,256,1024]{2,1,0:T(8,128)(2,1)} %constant.12.clone.table_ref, bf16[16,3072]{1,0:T(8,128)(2,1)} %get-tuple-element.17.rest_0_, ...), custom_call_target="tpu_custom_call" | custom-call | tf_op jit(solution)/shard_map/terms/pallas_call | solution.py:307
  33.1 28.5 %reduce.1 = (f32[2,16,600]{2,1,0:T(8,128)}, f32[16,128]{1,0:T(8,128)}, f32[8,128]{1,0:T(8,128)}) custom-call(f32[8,2,16,600]{3,2,1,0:T(8,128)} %get-tuple-element.21.dense_ref, f32[16,1]{1,0:T(8,128)} %get-tuple-element.22.cross_ref, f32[16,600]{1,0:T(8,128)} %reshape.24.field_ref, f32[1,16]{1,0:T(1,128)} %bitcast.4), custom_call_target="tpu_custom_call" | custom-call | tf_op jit(solution)/shard_map/reduce/pallas_call | solution.py:345
  61.7 1.7 %finish.1 = (f32[16,2,600]{2,1,0:T(2,128)}, f32[1,16]{1,0:T(1,128)}, f32[1,16]{1,0:T(1,128)}, f32[1,1]{1,0:T(1,128)}) custom-call(f32[2,16,600]{2,1,0:T(8,128)} %get-tuple-element.23.sums_ref, f32[16,128]{1,0:T(8,128)} %get-tuple-element.24.total_ref, f32[8,128]{1,0:T(8,128)} %get-tuple-element.25.mean_ref, f32[1,16]{1,0:T(1,128)} %bitcast.5), custom_call_target="tpu_custom_call" | custom-call | tf_op jit(solution)/shard_map/finish/pallas_call | solution.py:371
  (1 shorter events, 0.0 us)
Async XLA Ops:
  0.6 17.6 %copy-start = (f32[16,16,300]{2,1,0:T(8,128)S(1)}, f32[16,16,300]{2,1,0:T(8,128)}, u32[]{:S(2)}) copy-start(f32[16,16,300]{2,1,0:T(8,128)} %param.13) | copy-start | bytes 921604
  2.9 16.1 %collective-permute-start = (bf16[16,3072]{1,0:T(8,128)(2,1)}, bf16[16,3072]{1,0:T(8,128)(2,1)S(1)}, u32[]{:S(2)}, u32[]{:S(2)}) collective-permute-start(bf16[16,3072]{1,0:T(8,128)(2,1)} %get-tuple-element.18), channel_id=1, source_target_pairs={{0,1},{1,2},{2,3},{3,4},{4,5},{5,6},{6,7},{7,0},{8,9},{9,10},{10,1... | collective-permute-start | bytes 294920 | tf_op jit(solution)/shard_map/ppermute | solution.py:304
  5.9 13.1 %collective-permute-start.1 = (bf16[16,3072]{1,0:T(8,128)(2,1)}, bf16[16,3072]{1,0:T(8,128)(2,1)S(1)}, u32[]{:S(2)}, u32[]{:S(2)}) collective-permute-start(bf16[16,3072]{1,0:T(8,128)(2,1)} %get-tuple-element.19), channel_id=1, source_target_pairs={{0,7},{1,0},{2,1},{3,2},{4,3},{5,4},{6,5},{7,6},{8,15},{9,8},{10,9... | collective-permute-start | bytes 294920 | tf_op jit(solution)/shard_map/ppermute | solution.py:304
  8.9 10.1 %collective-permute-start.2 = (bf16[16,3072]{1,0:T(8,128)(2,1)}, bf16[16,3072]{1,0:T(8,128)(2,1)S(1)}, u32[]{:S(2)}, u32[]{:S(2)}) collective-permute-start(bf16[16,3072]{1,0:T(8,128)(2,1)} %get-tuple-element.20), channel_id=1, source_target_pairs={{0,4},{1,5},{2,6},{3,7},{4,0},{5,1},{6,2},{7,3},{8,12},{9,13},{10,... | collective-permute-start | bytes 294920 | tf_op jit(solution)/shard_map/ppermute | solution.py:304
  18.9 0.7 %copy-start.1 = (bf16[16,3072]{1,0:T(8,128)(2,1)}, bf16[16,3072]{1,0:T(8,128)(2,1)S(1)}, u32[]{:S(2)}) copy-start(bf16[16,3072]{1,0:T(8,128)(2,1)S(1)} %collective-permute-done.rest_1_) | copy-start | bytes 294916
  18.9 0.7 %copy-start.2 = (bf16[16,3072]{1,0:T(8,128)(2,1)}, bf16[16,3072]{1,0:T(8,128)(2,1)S(1)}, u32[]{:S(2)}) copy-start(bf16[16,3072]{1,0:T(8,128)(2,1)S(1)} %collective-permute-done.1.rest_2_) | copy-start | bytes 294916
  19.0 0.7 %copy-start.3 = (bf16[16,3072]{1,0:T(8,128)(2,1)}, bf16[16,3072]{1,0:T(8,128)(2,1)S(1)}, u32[]{:S(2)}) copy-start(bf16[16,3072]{1,0:T(8,128)(2,1)S(1)} %collective-permute-done.2.rest_3_) | copy-start | bytes 294916

commit v3 on v2

--- a/solution.py
+++ b/solution.py
@@ -168,11 +168,15 @@
     bias_ref,
     total_ref,
     mean_ref,
+    paired,
+    summed,
     landed,
     own_sums,
     other_sums,
     own_mean,
     other_mean,
+    pair_send,
+    pair_recv,
     share_send,
     share_recv,
     sum_send,
@@ -212,13 +216,41 @@
             copies.append(copy)
         return copies
 
-    shares = send_all(
-        lambda step: dense_ref.at[lax.rem(me + step, devices)], landed, share_send, share_recv, pb_peer, devices
-    )
+    parity, line = lax.rem(me, 2), me // 2
+    lines = devices // 2
+    order = [lines // 2] + [step for step in range(1, lines) if step != lines // 2] + [0]
+    pairs = {}
+    for step in order:
+        target = lax.rem(line + step, lines)
+        pairs[step] = pltpu.make_async_remote_copy(
+            src_ref=dense_ref.at[2 * target + 1 - parity],
+            dst_ref=paired.at[step],
+            send_sem=pair_send.at[step],
+            recv_sem=pair_recv.at[step],
+            device_id={"pb": 2 * line + 1 - parity},
+            device_id_type=pl.DeviceIdType.MESH,
+        )
+        pairs[step].start()
+    shares = {}
+    for step in order[:-1]:
+        owner = 2 * lax.rem(line + step, lines) + parity
+        pairs[step].wait_recv()
+        summed[step - 1] = dense_ref[owner] + paired[step]
+        shares[step] = pltpu.make_async_remote_copy(
+            src_ref=summed.at[step - 1],
+            dst_ref=landed.at[step - 1],
+            send_sem=share_send.at[step - 1],
+            recv_sem=share_recv.at[step - 1],
+            device_id={"pb": owner},
+            device_id_type=pl.DeviceIdType.MESH,
+        )
+        shares[step].start()
     weight = column_of(weight_ref[...])
-    real, imag = dense_ref[me, 0], dense_ref[me, 1]
-    for step in range(1, devices):
-        shares[step - 1].wait_recv()
+    pairs[0].wait_recv()
+    real = dense_ref[me, 0] + paired[0, 0]
+    imag = dense_ref[me, 1] + paired[0, 1]
+    for step in range(1, lines):
+        shares[step].wait_recv()
         real = real + landed[step - 1, 0]
         imag = imag + landed[step - 1, 1]
     bias_ref[0] = real
@@ -259,7 +291,7 @@
         arrived = other_mean[jnp.maximum(step - 1, 0)]
         total = total + jnp.where(step == 0, mean, arrived)
     mean_ref[...] = total
-    for copy in shares + sums + means:
+    for copy in list(pairs.values()) + list(shares.values()) + sums + means:
         copy.wait_send()
 
 
@@ -352,13 +384,17 @@
         in_specs=[vmem] * 4,
         out_specs=(vmem,) * 3,
         scratch_shapes=[
-            pltpu.VMEM((devices - 1, 2, walkers, width), F32),
+            pltpu.VMEM((devices // 2, 2, walkers, width), F32),
+            pltpu.VMEM((devices // 2 - 1, 2, walkers, width), F32),
+            pltpu.VMEM((devices // 2 - 1, 2, walkers, width), F32),
             pltpu.VMEM((walkers, 128), F32),
             pltpu.VMEM((devices - 1, walkers, 128), F32),
             pltpu.VMEM((8, 128), F32),
             pltpu.VMEM((groups - 1, 8, 128), F32),
-            pltpu.SemaphoreType.DMA((devices - 1,)),
-            pltpu.SemaphoreType.DMA((devices - 1,)),
+            pltpu.SemaphoreType.DMA((devices // 2,)),
+            pltpu.SemaphoreType.DMA((devices // 2,)),
+            pltpu.SemaphoreType.DMA((devices // 2 - 1,)),
+            pltpu.SemaphoreType.DMA((devices // 2 - 1,)),
             pltpu.SemaphoreType.DMA((devices - 1,)),
             pltpu.SemaphoreType.DMA((devices - 1,)),
             pltpu.SemaphoreType.DMA((groups - 1,)),

time: 63.6 us -> 58.4 us (0.918)
  Pallas kernels: 45.9 us -> 40.7 us
    pallas_call x1, Pallas kernels: 28.5 us -> 23.4 us  [local(): pl.pallas_call(functools.partial(reduce_kernel, devices, groups), out_sha...]
  transfers between devices with their start and end apart: 3 -> 3, of which waited for: 0 -> 0; matrix products, arithmetic and copies ran while one was open for 14% -> 16% of each run, Pallas kernels for 0% -> 0%
where the time goes in v3:
time: 58.4 us; the launch traced here: 58.2 us
  Pallas kernels  40.7 us (70%)
  local copies, waits for them, and re-layouts  9.78 us (17%)
  starting transfers between devices  6.99 us (12%)
  between operations  0.68 us (1%)
    pallas_call x1, Pallas kernels, local(): pl.pallas_call(functools.partial(reduce_kernel, devices, groups), out_sha...  23.4 us
    pallas_call x1, Pallas kernels, local(): pl.pallas_call(compute_kernel, grid=(slots,), out_shape=(jax.ShapeDtypeSt...  13.5 us
    unnamed x9, local copies, waits for them, and re-layouts  9.05 us
    ppermute x3, starting transfers between devices, local(): lax.ppermute(outgoing[slot], 'pb', [(i, (i + by) % devices) for i in rang...  6.99 us
    pallas_call x1, Pallas kernels, local(): pl.pallas_call(functools.partial(select_kernel, devices), out_shape=(jax....  2.21 us
    pallas_call x1, Pallas kernels, local(): pl.pallas_call(finish_kernel, out_shape=(jax.ShapeDtypeStruct((walkers, 2...  1.65 us
  transfers between devices with their start and end apart: 3, of which 0 were waited for; matrix products, arithmetic and copies ran while one was open for 16% of the time, Pallas kernels for 0%

profile of v3, /device:TPU:0, one launch (start us, length us, event | category | flops | bytes accessed | tf_op | source)
XLA Modules:
  0.0 58.2 jit_solution(13457478277589326865)
XLA Ops:
  0.6 0.0 copy-start
  0.6 2.2 %select.1 = (bf16[16,3072]{1,0:T(8,128)(2,1)}, bf16[16,3072]{1,0:T(8,128)(2,1)}, bf16[16,3072]{1,0:T(8,128)(2,1)}, bf16[16,3072]{1,0:T(8,128)(2,1)}) custom-call(s32[32]{0:T(128)} %source_ref.1, bf16[16,8,3072]{2,1,0:T(8,128)(2,1)} %greens_ref.1), custom_call_target="tpu_custom_call" | custom-call | tf_op jit(solution)/shard_map/select/pallas_call | solution.py:323
  2.9 3.0 %collective-permute-start = (bf16[16,3072]{1,0:T(8,128)(2,1)}, bf16[16,3072]{1,0:T(8,128)(2,1)S(1)}, u32[]{:S(2)}, u32[]{:S(2)}) collective-permute-start(bf16[16,3072]{1,0:T(8,128)(2,1)} %get-tuple-element.18), channel_id=1, source_target_pairs={{0,1},{1,2},{2,3},{3,4},{4,5},{5,6},{6,7},{7,0},{8,9},{9,10},{10,1... | collective-permute-start | bytes 294920 | tf_op jit(solution)/shard_map/ppermute | solution.py:336
  5.9 3.0 %collective-permute-start.1 = (bf16[16,3072]{1,0:T(8,128)(2,1)}, bf16[16,3072]{1,0:T(8,128)(2,1)S(1)}, u32[]{:S(2)}, u32[]{:S(2)}) collective-permute-start(bf16[16,3072]{1,0:T(8,128)(2,1)} %get-tuple-element.19), channel_id=1, source_target_pairs={{0,7},{1,0},{2,1},{3,2},{4,3},{5,4},{6,5},{7,6},{8,15},{9,8},{10,9... | collective-permute-start | bytes 294920 | tf_op jit(solution)/shard_map/ppermute | solution.py:336
  8.9 1.0 %collective-permute-start.2 = (bf16[16,3072]{1,0:T(8,128)(2,1)}, bf16[16,3072]{1,0:T(8,128)(2,1)S(1)}, u32[]{:S(2)}, u32[]{:S(2)}) collective-permute-start(bf16[16,3072]{1,0:T(8,128)(2,1)} %get-tuple-element.20), channel_id=1, source_target_pairs={{0,4},{1,5},{2,6},{3,7},{4,0},{5,1},{6,2},{7,3},{8,12},{9,13},{10,... | collective-permute-start | bytes 294920 | tf_op jit(solution)/shard_map/ppermute | solution.py:336
  9.8 8.3 %copy.13.chol_ref = bf16[4,300,3072]{2,1,0:T(8,128)(2,1)} copy(bf16[4,300,3072]{2,0,1:T(4,128)(2,1)} %param.9) | data formatting | bytes 14745600 | tf_op args[1]
  18.2 0.0 copy-done
  18.2 0.7 %reshape.24.field_ref = f32[16,600]{1,0:T(8,128)} reshape(f32[16,2,300]{2,1,0:T(2,128)S(1)} %constant_dynamic-slice_fusion) | data formatting | bytes 76800 | tf_op jit(solution)/shard_map/reshape | solution.py:372
  18.9 0.0 collective-permute-done.rest_1_
  18.9 0.0 copy-start.1
  18.9 0.0 collective-permute-done.1.rest_2_
  18.9 0.0 copy-start.2
  18.9 0.0 collective-permute-done.2.rest_3_
  19.0 0.0 copy-start.3
  19.0 0.6 %copy-done.1 = bf16[16,3072]{1,0:T(8,128)(2,1)} copy-done((bf16[16,3072]{1,0:T(8,128)(2,1)}, bf16[16,3072]{1,0:T(8,128)(2,1)S(1)}, u32[]{:S(2)}) %copy-start.1) | copy-done | bytes 98328
  19.6 0.0 copy-done.2
  19.6 0.1 copy-done.3
  19.7 13.5 %terms.1 = (f32[8,2,16,600]{3,2,1,0:T(8,128)}, f32[16,1]{1,0:T(8,128)}) custom-call(s32[4]{0:T(128)} %transfer_ref.1, s32[4]{0:T(128)} %multiple_ref.1, bf16[4,300,3072]{2,1,0:T(8,128)(2,1)} %copy.13.chol_ref, bf16[2,256,1024]{2,1,0:T(8,128)(2,1)} %constant.12.clone.table_ref, bf16[16,3072]{1,0:T(8,128)(2,1)} %get-tuple-element.17.rest_0_, ...), custom_call_target="tpu_custom_call" | custom-call | tf_op jit(solution)/shard_map/terms/pallas_call | solution.py:339
  33.1 23.4 %reduce.1 = (f32[2,16,600]{2,1,0:T(8,128)}, f32[16,128]{1,0:T(8,128)}, f32[8,128]{1,0:T(8,128)}) custom-call(f32[8,2,16,600]{3,2,1,0:T(8,128)} %get-tuple-element.21.dense_ref, f32[16,1]{1,0:T(8,128)} %get-tuple-element.22.cross_ref, f32[16,600]{1,0:T(8,128)} %reshape.24.field_ref, f32[1,16]{1,0:T(1,128)} %bitcast.4), custom_call_target="tpu_custom_call" | custom-call | tf_op jit(solution)/shard_map/reduce/pallas_call | solution.py:377
  56.5 1.7 %finish.1 = (f32[16,2,600]{2,1,0:T(2,128)}, f32[1,16]{1,0:T(1,128)}, f32[1,16]{1,0:T(1,128)}, f32[1,1]{1,0:T(1,128)}) custom-call(f32[2,16,600]{2,1,0:T(8,128)} %get-tuple-element.23.sums_ref, f32[16,128]{1,0:T(8,128)} %get-tuple-element.24.total_ref, f32[8,128]{1,0:T(8,128)} %get-tuple-element.25.mean_ref, f32[1,16]{1,0:T(1,128)} %bitcast.5), custom_call_target="tpu_custom_call" | custom-call | tf_op jit(solution)/shard_map/finish/pallas_call | solution.py:407
  (1 shorter events, 0.0 us)
Async XLA Ops:
  0.6 17.6 %copy-start = (f32[16,16,300]{2,1,0:T(8,128)S(1)}, f32[16,16,300]{2,1,0:T(8,128)}, u32[]{:S(2)}) copy-start(f32[16,16,300]{2,1,0:T(8,128)} %param.13) | copy-start | bytes 921604
  2.9 16.1 %collective-permute-start = (bf16[16,3072]{1,0:T(8,128)(2,1)}, bf16[16,3072]{1,0:T(8,128)(2,1)S(1)}, u32[]{:S(2)}, u32[]{:S(2)}) collective-permute-start(bf16[16,3072]{1,0:T(8,128)(2,1)} %get-tuple-element.18), channel_id=1, source_target_pairs={{0,1},{1,2},{2,3},{3,4},{4,5},{5,6},{6,7},{7,0},{8,9},{9,10},{10,1... | collective-permute-start | bytes 294920 | tf_op jit(solution)/shard_map/ppermute | solution.py:336
  5.9 13.1 %collective-permute-start.1 = (bf16[16,3072]{1,0:T(8,128)(2,1)}, bf16[16,3072]{1,0:T(8,128)(2,1)S(1)}, u32[]{:S(2)}, u32[]{:S(2)}) collective-permute-start(bf16[16,3072]{1,0:T(8,128)(2,1)} %get-tuple-element.19), channel_id=1, source_target_pairs={{0,7},{1,0},{2,1},{3,2},{4,3},{5,4},{6,5},{7,6},{8,15},{9,8},{10,9... | collective-permute-start | bytes 294920 | tf_op jit(solution)/shard_map/ppermute | solution.py:336
  8.9 10.1 %collective-permute-start.2 = (bf16[16,3072]{1,0:T(8,128)(2,1)}, bf16[16,3072]{1,0:T(8,128)(2,1)S(1)}, u32[]{:S(2)}, u32[]{:S(2)}) collective-permute-start(bf16[16,3072]{1,0:T(8,128)(2,1)} %get-tuple-element.20), channel_id=1, source_target_pairs={{0,4},{1,5},{2,6},{3,7},{4,0},{5,1},{6,2},{7,3},{8,12},{9,13},{10,... | collective-permute-start | bytes 294920 | tf_op jit(solution)/shard_map/ppermute | solution.py:336
  18.9 0.7 %copy-start.1 = (bf16[16,3072]{1,0:T(8,128)(2,1)}, bf16[16,3072]{1,0:T(8,128)(2,1)S(1)}, u32[]{:S(2)}) copy-start(bf16[16,3072]{1,0:T(8,128)(2,1)S(1)} %collective-permute-done.rest_1_) | copy-start | bytes 294916
  18.9 0.7 %copy-start.2 = (bf16[16,3072]{1,0:T(8,128)(2,1)}, bf16[16,3072]{1,0:T(8,128)(2,1)S(1)}, u32[]{:S(2)}) copy-start(bf16[16,3072]{1,0:T(8,128)(2,1)S(1)} %collective-permute-done.1.rest_2_) | copy-start | bytes 294916
  19.0 0.7 %copy-start.3 = (bf16[16,3072]{1,0:T(8,128)(2,1)}, bf16[16,3072]{1,0:T(8,128)(2,1)S(1)}, u32[]{:S(2)}) copy-start(bf16[16,3072]{1,0:T(8,128)(2,1)S(1)} %collective-permute-done.2.rest_3_) | copy-start | bytes 294916

commit v4 on v3

--- a/solution.py
+++ b/solution.py
@@ -90,7 +90,7 @@
                 at = (window * 2 + part) * WINDOW
                 operand[window, pl.ds(part * 2 * half + parity * half, half), :] = spread[:, at : at + WINDOW]
 
-    for i in range(OCCUPIED_COUNT):
+    def multiply(i):
         start = PAIR * (i // 2) + SHIFT * (i % 2)
         product[i] = lax.dot_general(
             operand[i % 2],
@@ -106,7 +106,10 @@
     off = [zero, zero]
     own = [zero, zero]
     trace = [zero, zero]
+    multiply(0)
     for i in range(OCCUPIED_COUNT):
+        if i + 1 < OCCUPIED_COUNT:
+            multiply(i + 1)
         for part in range(2):
             here = block(i, i, part)
             own[part] = own[part] + here * here

time: 58.4 us -> 58.4 us (level)
  no operation moved by 1% of the time
where the time goes in v4:
time: 58.4 us; the launch traced here: 58.2 us
  Pallas kernels  40.7 us (70%)
  local copies, waits for them, and re-layouts  9.78 us (17%)
  starting transfers between devices  6.99 us (12%)
  between operations  0.68 us (1%)
    pallas_call x1, Pallas kernels, local(): pl.pallas_call(functools.partial(reduce_kernel, devices, groups), out_sha...  23.4 us
    pallas_call x1, Pallas kernels, local(): pl.pallas_call(compute_kernel, grid=(slots,), out_shape=(jax.ShapeDtypeSt...  13.5 us
    unnamed x9, local copies, waits for them, and re-layouts  9.05 us
    ppermute x3, starting transfers between devices, local(): lax.ppermute(outgoing[slot], 'pb', [(i, (i + by) % devices) for i in rang...  6.99 us
    pallas_call x1, Pallas kernels, local(): pl.pallas_call(functools.partial(select_kernel, devices), out_shape=(jax....  2.21 us
    pallas_call x1, Pallas kernels, local(): pl.pallas_call(finish_kernel, out_shape=(jax.ShapeDtypeStruct((walkers, 2...  1.65 us
  transfers between devices with their start and end apart: 3, of which 0 were waited for; matrix products, arithmetic and copies ran while one was open for 16% of the time, Pallas kernels for 0%

profile of v4, /device:TPU:0, one launch (start us, length us, event | category | flops | bytes accessed | tf_op | source)
XLA Modules:
  0.0 58.2 jit_solution(13457478277589326865)
XLA Ops:
  0.6 0.0 copy-start
  0.6 2.2 %select.1 = (bf16[16,3072]{1,0:T(8,128)(2,1)}, bf16[16,3072]{1,0:T(8,128)(2,1)}, bf16[16,3072]{1,0:T(8,128)(2,1)}, bf16[16,3072]{1,0:T(8,128)(2,1)}) custom-call(s32[32]{0:T(128)} %source_ref.1, bf16[16,8,3072]{2,1,0:T(8,128)(2,1)} %greens_ref.1), custom_call_target="tpu_custom_call" | custom-call | tf_op jit(solution)/shard_map/select/pallas_call | solution.py:326
  2.9 3.0 %collective-permute-start = (bf16[16,3072]{1,0:T(8,128)(2,1)}, bf16[16,3072]{1,0:T(8,128)(2,1)S(1)}, u32[]{:S(2)}, u32[]{:S(2)}) collective-permute-start(bf16[16,3072]{1,0:T(8,128)(2,1)} %get-tuple-element.18), channel_id=1, source_target_pairs={{0,1},{1,2},{2,3},{3,4},{4,5},{5,6},{6,7},{7,0},{8,9},{9,10},{10,1... | collective-permute-start | bytes 294920 | tf_op jit(solution)/shard_map/ppermute | solution.py:339
  5.9 3.0 %collective-permute-start.1 = (bf16[16,3072]{1,0:T(8,128)(2,1)}, bf16[16,3072]{1,0:T(8,128)(2,1)S(1)}, u32[]{:S(2)}, u32[]{:S(2)}) collective-permute-start(bf16[16,3072]{1,0:T(8,128)(2,1)} %get-tuple-element.19), channel_id=1, source_target_pairs={{0,7},{1,0},{2,1},{3,2},{4,3},{5,4},{6,5},{7,6},{8,15},{9,8},{10,9... | collective-permute-start | bytes 294920 | tf_op jit(solution)/shard_map/ppermute | solution.py:339
  8.9 1.0 %collective-permute-start.2 = (bf16[16,3072]{1,0:T(8,128)(2,1)}, bf16[16,3072]{1,0:T(8,128)(2,1)S(1)}, u32[]{:S(2)}, u32[]{:S(2)}) collective-permute-start(bf16[16,3072]{1,0:T(8,128)(2,1)} %get-tuple-element.20), channel_id=1, source_target_pairs={{0,4},{1,5},{2,6},{3,7},{4,0},{5,1},{6,2},{7,3},{8,12},{9,13},{10,... | collective-permute-start | bytes 294920 | tf_op jit(solution)/shard_map/ppermute | solution.py:339
  9.8 8.3 %copy.13.chol_ref = bf16[4,300,3072]{2,1,0:T(8,128)(2,1)} copy(bf16[4,300,3072]{2,0,1:T(4,128)(2,1)} %param.9) | data formatting | bytes 14745600 | tf_op args[1]
  18.2 0.0 copy-done
  18.2 0.7 %reshape.24.field_ref = f32[16,600]{1,0:T(8,128)} reshape(f32[16,2,300]{2,1,0:T(2,128)S(1)} %constant_dynamic-slice_fusion) | data formatting | bytes 76800 | tf_op jit(solution)/shard_map/reshape | solution.py:375
  18.9 0.0 collective-permute-done.rest_1_
  18.9 0.0 copy-start.1
  18.9 0.0 collective-permute-done.1.rest_2_
  18.9 0.0 copy-start.2
  18.9 0.0 collective-permute-done.2.rest_3_
  19.0 0.0 copy-start.3
  19.0 0.6 %copy-done.1 = bf16[16,3072]{1,0:T(8,128)(2,1)} copy-done((bf16[16,3072]{1,0:T(8,128)(2,1)}, bf16[16,3072]{1,0:T(8,128)(2,1)S(1)}, u32[]{:S(2)}) %copy-start.1) | copy-done | bytes 98328
  19.6 0.0 copy-done.2
  19.6 0.1 copy-done.3
  19.7 13.5 %terms.1 = (f32[8,2,16,600]{3,2,1,0:T(8,128)}, f32[16,1]{1,0:T(8,128)}) custom-call(s32[4]{0:T(128)} %transfer_ref.1, s32[4]{0:T(128)} %multiple_ref.1, bf16[4,300,3072]{2,1,0:T(8,128)(2,1)} %copy.13.chol_ref, bf16[2,256,1024]{2,1,0:T(8,128)(2,1)} %constant.12.clone.table_ref, bf16[16,3072]{1,0:T(8,128)(2,1)} %get-tuple-element.17.rest_0_, ...), custom_call_target="tpu_custom_call" | custom-call | tf_op jit(solution)/shard_map/terms/pallas_call | solution.py:342
  33.1 23.4 %reduce.1 = (f32[2,16,600]{2,1,0:T(8,128)}, f32[16,128]{1,0:T(8,128)}, f32[8,128]{1,0:T(8,128)}) custom-call(f32[8,2,16,600]{3,2,1,0:T(8,128)} %get-tuple-element.21.dense_ref, f32[16,1]{1,0:T(8,128)} %get-tuple-element.22.cross_ref, f32[16,600]{1,0:T(8,128)} %reshape.24.field_ref, f32[1,16]{1,0:T(1,128)} %bitcast.4), custom_call_target="tpu_custom_call" | custom-call | tf_op jit(solution)/shard_map/reduce/pallas_call | solution.py:380
  56.5 1.7 %finish.1 = (f32[16,2,600]{2,1,0:T(2,128)}, f32[1,16]{1,0:T(1,128)}, f32[1,16]{1,0:T(1,128)}, f32[1,1]{1,0:T(1,128)}) custom-call(f32[2,16,600]{2,1,0:T(8,128)} %get-tuple-element.23.sums_ref, f32[16,128]{1,0:T(8,128)} %get-tuple-element.24.total_ref, f32[8,128]{1,0:T(8,128)} %get-tuple-element.25.mean_ref, f32[1,16]{1,0:T(1,128)} %bitcast.5), custom_call_target="tpu_custom_call" | custom-call | tf_op jit(solution)/shard_map/finish/pallas_call | solution.py:410
  (1 shorter events, 0.0 us)
Async XLA Ops:
  0.6 17.6 %copy-start = (f32[16,16,300]{2,1,0:T(8,128)S(1)}, f32[16,16,300]{2,1,0:T(8,128)}, u32[]{:S(2)}) copy-start(f32[16,16,300]{2,1,0:T(8,128)} %param.13) | copy-start | bytes 921604
  2.9 16.1 %collective-permute-start = (bf16[16,3072]{1,0:T(8,128)(2,1)}, bf16[16,3072]{1,0:T(8,128)(2,1)S(1)}, u32[]{:S(2)}, u32[]{:S(2)}) collective-permute-start(bf16[16,3072]{1,0:T(8,128)(2,1)} %get-tuple-element.18), channel_id=1, source_target_pairs={{0,1},{1,2},{2,3},{3,4},{4,5},{5,6},{6,7},{7,0},{8,9},{9,10},{10,1... | collective-permute-start | bytes 294920 | tf_op jit(solution)/shard_map/ppermute | solution.py:339
  5.9 13.1 %collective-permute-start.1 = (bf16[16,3072]{1,0:T(8,128)(2,1)}, bf16[16,3072]{1,0:T(8,128)(2,1)S(1)}, u32[]{:S(2)}, u32[]{:S(2)}) collective-permute-start(bf16[16,3072]{1,0:T(8,128)(2,1)} %get-tuple-element.19), channel_id=1, source_target_pairs={{0,7},{1,0},{2,1},{3,2},{4,3},{5,4},{6,5},{7,6},{8,15},{9,8},{10,9... | collective-permute-start | bytes 294920 | tf_op jit(solution)/shard_map/ppermute | solution.py:339
  8.9 10.1 %collective-permute-start.2 = (bf16[16,3072]{1,0:T(8,128)(2,1)}, bf16[16,3072]{1,0:T(8,128)(2,1)S(1)}, u32[]{:S(2)}, u32[]{:S(2)}) collective-permute-start(bf16[16,3072]{1,0:T(8,128)(2,1)} %get-tuple-element.20), channel_id=1, source_target_pairs={{0,4},{1,5},{2,6},{3,7},{4,0},{5,1},{6,2},{7,3},{8,12},{9,13},{10,... | collective-permute-start | bytes 294920 | tf_op jit(solution)/shard_map/ppermute | solution.py:339
  18.9 0.7 %copy-start.1 = (bf16[16,3072]{1,0:T(8,128)(2,1)}, bf16[16,3072]{1,0:T(8,128)(2,1)S(1)}, u32[]{:S(2)}) copy-start(bf16[16,3072]{1,0:T(8,128)(2,1)S(1)} %collective-permute-done.rest_1_) | copy-start | bytes 294916
  18.9 0.7 %copy-start.2 = (bf16[16,3072]{1,0:T(8,128)(2,1)}, bf16[16,3072]{1,0:T(8,128)(2,1)S(1)}, u32[]{:S(2)}) copy-start(bf16[16,3072]{1,0:T(8,128)(2,1)S(1)} %collective-permute-done.1.rest_2_) | copy-start | bytes 294916
  19.0 0.7 %copy-start.3 = (bf16[16,3072]{1,0:T(8,128)(2,1)}, bf16[16,3072]{1,0:T(8,128)(2,1)S(1)}, u32[]{:S(2)}) copy-start(bf16[16,3072]{1,0:T(8,128)(2,1)S(1)} %collective-permute-done.2.rest_3_) | copy-start | bytes 294916

commit v5 on v4

--- a/solution.py
+++ b/solution.py
@@ -17,6 +17,7 @@
 PAIR = 2 * DOUBLED
 WINDOW = 256
 SHIFT = PAIR - WINDOW
+LANES = 128
 VMEM_LIMIT = 60 * 1024 * 1024
 F32 = jnp.float32
 
@@ -64,7 +65,7 @@
 def compute_kernel(
     transfer_ref, multiple_ref, chol_ref, table_ref, *rest
 ):
-    greens, (dense_ref, cross_ref, operand, product, diagonal, crossed, green) = rest[:-7], rest[-7:]
+    greens, (dense_ref, cross_ref, operand, product, diagonal, crossed, green, tails) = rest[:-8], rest[-8:]
     slot = pl.program_id(0)
     slots = pl.num_programs(0)
     walkers = green.shape[0]
@@ -90,19 +91,34 @@
                 at = (window * 2 + part) * WINDOW
                 operand[window, pl.ds(part * 2 * half + parity * half, half), :] = spread[:, at : at + WINDOW]
 
+    main = vectors // WINDOW * WINDOW
+    rest_count = vectors - main
+
+    @pl.when(slot == 0)
+    def _():
+        tails[...] = jnp.zeros_like(tails)
+
+    def window_of(i):
+        start = PAIR * (i // 2) + SHIFT * (i % 2)
+        return slice(start, start + WINDOW)
+
+    def times(parity, right):
+        return lax.dot_general(operand[parity], right, (((1,), (1,)), ((), ())), preferred_element_type=F32)
+
+    for i in range(OCCUPIED_COUNT):
+        tails[i % 2, pl.ds(LANES * (i // 2), rest_count), :] = chol_ref[0, main:vectors, window_of(i)]
+    for parity in range(2):
+        ends = times(parity, tails[parity])
+        for p in range(pairs):
+            product[2 * p + parity, :, main : main + LANES] = ends[:, LANES * p : LANES * (p + 1)]
+
     def multiply(i):
-        start = PAIR * (i // 2) + SHIFT * (i % 2)
-        product[i] = lax.dot_general(
-            operand[i % 2],
-            chol_ref[0, :, start : start + WINDOW],
-            (((1,), (1,)), ((), ())),
-            preferred_element_type=F32,
-        )
+        product[i, :, :main] = times(i % 2, chol_ref[0, :main, window_of(i)])
 
     def block(i, j, part):
         return product[i, pl.ds(row_of(part, j, walkers), walkers), :]
 
-    zero = jnp.zeros((walkers, vectors), F32)
+    zero = jnp.zeros((walkers, main + LANES), F32)
     off = [zero, zero]
     own = [zero, zero]
     trace = [zero, zero]
@@ -117,8 +133,8 @@
             for j in range(i):
                 off[part] = off[part] + block(i, j, part) * block(j, i, part)
     for part in range(2):
-        diagonal[slot, part] = scaled * trace[part]
-    total = scaled * ((own[0] - own[1]) + 2.0 * (off[0] - off[1]))
+        diagonal[slot, part] = scaled * trace[part][:, :vectors]
+    total = scaled * ((own[0] - own[1]) + 2.0 * (off[0] - off[1]))[:, :vectors]
 
     @pl.when(slot == 0)
     def _():
@@ -359,10 +375,11 @@
         ),
         scratch_shapes=[
             pltpu.VMEM((2, rows, WINDOW), greens.dtype),
-            pltpu.VMEM((OCCUPIED_COUNT, rows, vectors), F32),
+            pltpu.VMEM((OCCUPIED_COUNT, rows, vectors // WINDOW * WINDOW + LANES), F32),
             pltpu.VMEM((slots, 2, walkers, vectors), F32),
             pltpu.VMEM((walkers, vectors), F32),
             pltpu.VMEM((walkers, flat), greens.dtype),
+            pltpu.VMEM((2, LANES * OCCUPIED_COUNT // 2, WINDOW), greens.dtype),
         ],
         compiler_params=pltpu.CompilerParams(
             dimension_semantics=("arbitrary",), vmem_limit_bytes=VMEM_LIMIT

time: 58.4 us -> 56.9 us (0.974)
  Pallas kernels: 40.7 us -> 39.2 us
    pallas_call x1, Pallas kernels: 13.5 us -> 11.9 us  [local(): pl.pallas_call(compute_kernel, grid=(slots,), out_shape=(jax.ShapeDtypeSt...]
where the time goes in v5:
time: 56.9 us; the launch traced here: 56.6 us
  Pallas kernels  39.2 us (69%)
  local copies, waits for them, and re-layouts  9.78 us (17%)
  starting transfers between devices  6.99 us (12%)
  between operations  0.68 us (1%)
    pallas_call x1, Pallas kernels, local(): pl.pallas_call(functools.partial(reduce_kernel, devices, groups), out_sha...  23.4 us
    pallas_call x1, Pallas kernels, local(): pl.pallas_call(compute_kernel, grid=(slots,), out_shape=(jax.ShapeDtypeSt...  11.9 us
    unnamed x9, local copies, waits for them, and re-layouts  9.05 us
    ppermute x3, starting transfers between devices, local(): lax.ppermute(outgoing[slot], 'pb', [(i, (i + by) % devices) for i in rang...  6.99 us
    pallas_call x1, Pallas kernels, local(): pl.pallas_call(functools.partial(select_kernel, devices), out_shape=(jax....  2.21 us
    pallas_call x1, Pallas kernels, local(): pl.pallas_call(finish_kernel, out_shape=(jax.ShapeDtypeStruct((walkers, 2...  1.65 us
  transfers between devices with their start and end apart: 3, of which 0 were waited for; matrix products, arithmetic and copies ran while one was open for 16% of the time, Pallas kernels for 0%

profile of v5, /device:TPU:0, one launch (start us, length us, event | category | flops | bytes accessed | tf_op | source)
XLA Modules:
  0.0 56.6 jit_solution(9582072653688411471)
XLA Ops:
  0.6 0.0 copy-start
  0.6 2.2 %select.1 = (bf16[16,3072]{1,0:T(8,128)(2,1)}, bf16[16,3072]{1,0:T(8,128)(2,1)}, bf16[16,3072]{1,0:T(8,128)(2,1)}, bf16[16,3072]{1,0:T(8,128)(2,1)}) custom-call(s32[32]{0:T(128)} %source_ref.1, bf16[16,8,3072]{2,1,0:T(8,128)(2,1)} %greens_ref.1), custom_call_target="tpu_custom_call" | custom-call | tf_op jit(solution)/shard_map/select/pallas_call | solution.py:342
  2.9 3.0 %collective-permute-start = (bf16[16,3072]{1,0:T(8,128)(2,1)}, bf16[16,3072]{1,0:T(8,128)(2,1)S(1)}, u32[]{:S(2)}, u32[]{:S(2)}) collective-permute-start(bf16[16,3072]{1,0:T(8,128)(2,1)} %get-tuple-element.18), channel_id=1, source_target_pairs={{0,1},{1,2},{2,3},{3,4},{4,5},{5,6},{6,7},{7,0},{8,9},{9,10},{10,1... | collective-permute-start | bytes 294920 | tf_op jit(solution)/shard_map/ppermute | solution.py:355
  5.9 3.0 %collective-permute-start.1 = (bf16[16,3072]{1,0:T(8,128)(2,1)}, bf16[16,3072]{1,0:T(8,128)(2,1)S(1)}, u32[]{:S(2)}, u32[]{:S(2)}) collective-permute-start(bf16[16,3072]{1,0:T(8,128)(2,1)} %get-tuple-element.19), channel_id=1, source_target_pairs={{0,7},{1,0},{2,1},{3,2},{4,3},{5,4},{6,5},{7,6},{8,15},{9,8},{10,9... | collective-permute-start | bytes 294920 | tf_op jit(solution)/shard_map/ppermute | solution.py:355
  8.9 1.0 %collective-permute-start.2 = (bf16[16,3072]{1,0:T(8,128)(2,1)}, bf16[16,3072]{1,0:T(8,128)(2,1)S(1)}, u32[]{:S(2)}, u32[]{:S(2)}) collective-permute-start(bf16[16,3072]{1,0:T(8,128)(2,1)} %get-tuple-element.20), channel_id=1, source_target_pairs={{0,4},{1,5},{2,6},{3,7},{4,0},{5,1},{6,2},{7,3},{8,12},{9,13},{10,... | collective-permute-start | bytes 294920 | tf_op jit(solution)/shard_map/ppermute | solution.py:355
  9.8 8.3 %copy.13.chol_ref = bf16[4,300,3072]{2,1,0:T(8,128)(2,1)} copy(bf16[4,300,3072]{2,0,1:T(4,128)(2,1)} %param.9) | data formatting | bytes 14745600 | tf_op args[1]
  18.2 0.0 copy-done
  18.2 0.7 %reshape.24.field_ref = f32[16,600]{1,0:T(8,128)} reshape(f32[16,2,300]{2,1,0:T(2,128)S(1)} %constant_dynamic-slice_fusion) | data formatting | bytes 76800 | tf_op jit(solution)/shard_map/reshape | solution.py:392
  18.9 0.0 collective-permute-done.rest_1_
  18.9 0.0 copy-start.1
  18.9 0.0 collective-permute-done.1.rest_2_
  18.9 0.0 copy-start.2
  18.9 0.0 collective-permute-done.2.rest_3_
  19.0 0.0 copy-start.3
  19.0 0.6 %copy-done.1 = bf16[16,3072]{1,0:T(8,128)(2,1)} copy-done((bf16[16,3072]{1,0:T(8,128)(2,1)}, bf16[16,3072]{1,0:T(8,128)(2,1)S(1)}, u32[]{:S(2)}) %copy-start.1) | copy-done | bytes 98328
  19.6 0.0 copy-done.2
  19.6 0.1 copy-done.3
  19.7 11.9 %terms.1 = (f32[8,2,16,600]{3,2,1,0:T(8,128)}, f32[16,1]{1,0:T(8,128)}) custom-call(s32[4]{0:T(128)} %transfer_ref.1, s32[4]{0:T(128)} %multiple_ref.1, bf16[4,300,3072]{2,1,0:T(8,128)(2,1)} %copy.13.chol_ref, bf16[2,256,1024]{2,1,0:T(8,128)(2,1)} %constant.12.clone.table_ref, bf16[16,3072]{1,0:T(8,128)(2,1)} %get-tuple-element.17.rest_0_, ...), custom_call_target="tpu_custom_call" | custom-call | tf_op jit(solution)/shard_map/terms/pallas_call | solution.py:358
  31.6 23.4 %reduce.1 = (f32[2,16,600]{2,1,0:T(8,128)}, f32[16,128]{1,0:T(8,128)}, f32[8,128]{1,0:T(8,128)}) custom-call(f32[8,2,16,600]{3,2,1,0:T(8,128)} %get-tuple-element.21.dense_ref, f32[16,1]{1,0:T(8,128)} %get-tuple-element.22.cross_ref, f32[16,600]{1,0:T(8,128)} %reshape.24.field_ref, f32[1,16]{1,0:T(1,128)} %bitcast.4), custom_call_target="tpu_custom_call" | custom-call | tf_op jit(solution)/shard_map/reduce/pallas_call | solution.py:397
  55.0 1.7 %finish.1 = (f32[16,2,600]{2,1,0:T(2,128)}, f32[1,16]{1,0:T(1,128)}, f32[1,16]{1,0:T(1,128)}, f32[1,1]{1,0:T(1,128)}) custom-call(f32[2,16,600]{2,1,0:T(8,128)} %get-tuple-element.23.sums_ref, f32[16,128]{1,0:T(8,128)} %get-tuple-element.24.total_ref, f32[8,128]{1,0:T(8,128)} %get-tuple-element.25.mean_ref, f32[1,16]{1,0:T(1,128)} %bitcast.5), custom_call_target="tpu_custom_call" | custom-call | tf_op jit(solution)/shard_map/finish/pallas_call | solution.py:427
  (1 shorter events, 0.0 us)
Async XLA Ops:
  0.6 17.6 %copy-start = (f32[16,16,300]{2,1,0:T(8,128)S(1)}, f32[16,16,300]{2,1,0:T(8,128)}, u32[]{:S(2)}) copy-start(f32[16,16,300]{2,1,0:T(8,128)} %param.13) | copy-start | bytes 921604
  2.9 16.1 %collective-permute-start = (bf16[16,3072]{1,0:T(8,128)(2,1)}, bf16[16,3072]{1,0:T(8,128)(2,1)S(1)}, u32[]{:S(2)}, u32[]{:S(2)}) collective-permute-start(bf16[16,3072]{1,0:T(8,128)(2,1)} %get-tuple-element.18), channel_id=1, source_target_pairs={{0,1},{1,2},{2,3},{3,4},{4,5},{5,6},{6,7},{7,0},{8,9},{9,10},{10,1... | collective-permute-start | bytes 294920 | tf_op jit(solution)/shard_map/ppermute | solution.py:355
  5.9 13.1 %collective-permute-start.1 = (bf16[16,3072]{1,0:T(8,128)(2,1)}, bf16[16,3072]{1,0:T(8,128)(2,1)S(1)}, u32[]{:S(2)}, u32[]{:S(2)}) collective-permute-start(bf16[16,3072]{1,0:T(8,128)(2,1)} %get-tuple-element.19), channel_id=1, source_target_pairs={{0,7},{1,0},{2,1},{3,2},{4,3},{5,4},{6,5},{7,6},{8,15},{9,8},{10,9... | collective-permute-start | bytes 294920 | tf_op jit(solution)/shard_map/ppermute | solution.py:355
  8.9 10.1 %collective-permute-start.2 = (bf16[16,3072]{1,0:T(8,128)(2,1)}, bf16[16,3072]{1,0:T(8,128)(2,1)S(1)}, u32[]{:S(2)}, u32[]{:S(2)}) collective-permute-start(bf16[16,3072]{1,0:T(8,128)(2,1)} %get-tuple-element.20), channel_id=1, source_target_pairs={{0,4},{1,5},{2,6},{3,7},{4,0},{5,1},{6,2},{7,3},{8,12},{9,13},{10,... | collective-permute-start | bytes 294920 | tf_op jit(solution)/shard_map/ppermute | solution.py:355
  18.9 0.7 %copy-start.1 = (bf16[16,3072]{1,0:T(8,128)(2,1)}, bf16[16,3072]{1,0:T(8,128)(2,1)S(1)}, u32[]{:S(2)}) copy-start(bf16[16,3072]{1,0:T(8,128)(2,1)S(1)} %collective-permute-done.rest_1_) | copy-start | bytes 294916
  18.9 0.7 %copy-start.2 = (bf16[16,3072]{1,0:T(8,128)(2,1)}, bf16[16,3072]{1,0:T(8,128)(2,1)S(1)}, u32[]{:S(2)}) copy-start(bf16[16,3072]{1,0:T(8,128)(2,1)S(1)} %collective-permute-done.1.rest_2_) | copy-start | bytes 294916
  19.0 0.7 %copy-start.3 = (bf16[16,3072]{1,0:T(8,128)(2,1)}, bf16[16,3072]{1,0:T(8,128)(2,1)S(1)}, u32[]{:S(2)}) copy-start(bf16[16,3072]{1,0:T(8,128)(2,1)S(1)} %collective-permute-done.2.rest_3_) | copy-start | bytes 294916
